TPU v7x, 256 devices: a whole 4x4x8 slice. The times are simulated.
256 devices in a mesh: ctx: 32 (over x, z), head: 8 (over y, core).
Axes of the slice: x: 4, y: 4, z: 8, core: 2. Of those that a mesh axis runs over, the one named last changes fastest.
Arguments:
- keys: bfloat16 [65536, 5120], P('ctx', 'head'), may hold values from -6 to 6
- values: bfloat16 [65536, 5120], P('ctx', 'head'), may hold values from -6 to 6
- queries: bfloat16 [65536, 5120], P('ctx', 'head'), may hold values from -6 to 6
- rates: float32 [65536, 16], P('ctx', 'head'), may hold values from 9.765625e-05 to 0.0009765625
- w_gate: bfloat16 [320, 16, 320], P('ctx', 'head'), may hold values from -0.3125 to 0.3125
- w_up: bfloat16 [320, 16, 320], P('ctx', 'head'), may hold values from -0.3125 to 0.3125
- w_down: bfloat16 [320, 16, 320], P('ctx', 'head'), may hold values from -0.3125 to 0.3125
- gain: float32 [5120], P('head'), may hold values from 0.5 to 1.5
Outputs:
- output: bfloat16 [65536, 5120], P('ctx', 'head')
- new_gate: bfloat16 [320, 16, 320], P('ctx', 'head')
- new_up: bfloat16 [320, 16, 320], P('ctx', 'head')
- new_down: bfloat16 [320, 16, 320], P('ctx', 'head')
All inputs are finite; a program needn't handle non-finite values.
Results may differ from a plain program's by a relative error of at most 0.0092.
Values may be sent and summed in bfloat16 or wider, within the bound.
No kernel may reach another device: no remote copies, remote signals or barrier semaphores. Data moves between devices by JAX's collectives and lax.ppermute only.
A program may use at most 128 MiB of HBM per device.

v0:
```python
import jax
import jax.numpy as jnp
from jax import lax
from jax.sharding import PartitionSpec as P

HEADS = 16
DH = 320


EPS = 1e-06


def joined_along(pieces, dim):
    dims = list(pieces.shape[1:])
    dims[dim] *= pieces.shape[0]
    return jnp.moveaxis(pieces, 0, dim).reshape(dims)


def from_everyone(array, axis):
    peers = lax.axis_size(axis)
    return lax.all_to_all(
        jnp.broadcast_to(array[None], (peers, *array.shape)), axis, 0, 0, tiled=True
    )


def gather_directly(array, axis, dim):
    return joined_along(from_everyone(array, axis), dim)


def sent_together(arrays, axis, dim, along):
    ends, at = ([], 0)
    for a in arrays[:-1]:
        at += a.shape[along]
        ends.append(at)
    both = jnp.concatenate(arrays, axis=along)
    return tuple(jnp.split(gather_directly(both, axis, dim), ends, axis=along))


def taken_together(array, axis):
    everything = from_everyone(array, axis)
    return jnp.sum(everything, axis=0)


def per_device(keys, values, queries, rates, w_gate, w_up, w_down, gain):
    rows = keys.shape[0]
    heads = w_gate.shape[1]
    width = w_gate.shape[2]
    local_units = w_gate.shape[0]
    keyh = keys.reshape(rows, heads, width)
    valueh = values.reshape(rows, heads, width)
    queryh = queries.reshape(rows, heads, width)
    full_gate, full_up, full_down = sent_together((w_gate, w_up, w_down), "ctx", 0, 1)
    gpre = jnp.einsum("thd,fhd->thf", keyh, full_gate, preferred_element_type=jnp.float32)
    upre = jnp.einsum("thd,fhd->thf", keyh, full_up, preferred_element_type=jnp.float32)
    sig = jax.nn.sigmoid(gpre)
    act = gpre * sig
    slope = sig * (1.0 + gpre * (1.0 - sig))
    hidden = (act * upre).astype(jnp.bfloat16)
    scaled = (valueh.astype(jnp.float32) * rates[:, :, None]).astype(jnp.bfloat16)
    back = jnp.einsum("thd,fhd->thf", scaled, full_down, preferred_element_type=jnp.float32)
    dgate = (back * upre * slope).astype(jnp.bfloat16)
    dup = (back * act).astype(jnp.bfloat16)
    grad_gate = jnp.einsum("thf,thd->fhd", dgate, keyh, preferred_element_type=jnp.float32)
    grad_up = jnp.einsum("thf,thd->fhd", dup, keyh, preferred_element_type=jnp.float32)
    grad_down = jnp.einsum("thf,thd->fhd", hidden, scaled, preferred_element_type=jnp.float32)
    total = lax.psum(jnp.stack([grad_gate, grad_up, grad_down], axis=1), "ctx")
    olds = jnp.stack([full_gate, full_up, full_down], axis=1).astype(jnp.float32)
    updated = olds + total
    old_sq = jnp.sum(olds * olds, axis=0)
    new_sq = jnp.sum(updated * updated, axis=0)
    fresh = (updated * (jnp.sqrt(old_sq) * lax.rsqrt(new_sq + EPS))[None]).astype(jnp.bfloat16)
    offset = lax.axis_index("ctx") * local_units
    mine = lax.dynamic_slice_in_dim(fresh, offset, local_units, 0)
    new_gate = fresh[:, 0]
    new_up = fresh[:, 1]
    new_down = fresh[:, 2]
    qgate = jnp.einsum("thd,fhd->thf", queryh, new_gate, preferred_element_type=jnp.float32)
    qup = jnp.einsum("thd,fhd->thf", queryh, new_up, preferred_element_type=jnp.float32)
    mixed = (jax.nn.silu(qgate) * qup).astype(jnp.bfloat16)
    outh = jnp.einsum("thf,fhd->thd", mixed, new_down, preferred_element_type=jnp.float32)
    squares = taken_together(jnp.sum(outh * outh, axis=(1, 2)), "head")
    scale = lax.rsqrt(squares / (HEADS * DH) + EPS)
    result = outh * scale[:, None, None] * gain.reshape(heads, width)[None]
    output = result.reshape(rows, heads * width).astype(jnp.bfloat16)
    return (output, mine[:, 0], mine[:, 1], mine[:, 2])


def solution(mesh):
    in_specs = (
        P("ctx", "head"),
        P("ctx", "head"),
        P("ctx", "head"),
        P("ctx", "head"),
        P("ctx", "head", None),
        P("ctx", "head", None),
        P("ctx", "head", None),
        P("head"),
    )
    out_specs = (
        P("ctx", "head"),
        P("ctx", "head", None),
        P("ctx", "head", None),
        P("ctx", "head", None),
    )
    return jax.shard_map(
        per_device, mesh=mesh, in_specs=in_specs, out_specs=out_specs, check_vma=False
    )
```

profile of v0, /device:TPU:2, one launch (start us, length us, event | category | flops | bytes accessed | tf_op | source)
XLA Modules:
  0.0 290.8 jit_solution(10349840413681517928)
XLA Ops:
  8.0 1.4 broadcast_in_dim.4
  9.4 11.7 %all-to-all-start = ((bf16[32,10,6,320]{3,2,1,0:T(8,128)(2,1)}), bf16[32,10,6,320]{3,2,1,0:T(8,128)(2,1)}, u32[]{:S(2)}, u32[]{:S(2)}) async-start(bf16[32,10,6,320]{3,2,1,0:T(8,128)(2,1)} %broadcast_in_dim.4), calls=%async_computation | async-start | bytes 3932160 | tf_op jit(solution)/shard_map/all_to_all | solution.py:21
  21.1 3.0 %copy.53 = bf16[2048,640]{0,1:T(8,128)(2,1)S(1)} copy(bf16[2048,640]{1,0:T(8,128)(2,1)} %param.8) | data formatting | bytes 5242880 | tf_op args[0]
  24.1 4.4 %copy.52 = bf16[2048,640]{0,1:T(8,128)(2,1)} copy(bf16[2048,640]{1,0:T(8,128)(2,1)} %param.9) | data formatting | bytes 5242880 | tf_op args[1]
  28.5 37.3 %all-to-all-done = bf16[32,10,6,320]{3,2,1,0:T(8,128)(2,1)} async-done(((bf16[32,10,6,320]{3,2,1,0:T(8,128)(2,1)}), bf16[32,10,6,320]{3,2,1,0:T(8,128)(2,1)}, u32[]{:S(2)}, u32[]{:S(2)}) %all-to-all-start) | async-done | bytes 1228832 | tf_op jit(solution)/shard_map/all_to_all | solution.py:21
  65.8 4.1 %fusion.46 = (bf16[320,2,320]{2,1,0:T(2,128)(2,1)S(1)}, bf16[320,2,320]{2,1,0:T(2,128)(2,1)S(1)}, bf16[320,2,320]{2,1,0:T(2,128)(2,1)S(1)}) fusion(bf16[320,6,320]{2,1,0:T(8,128)(2,1)} %bitcast), kind=kLoop, calls=%fused_computation.63 | loop fusion | bytes 2457600 | tf_op jit(solution)/shard_map/split | solution.py:36
  70.0 1.5 fusion.40
  71.6 3.8 %fusion.38 = f32[2,320,2048]{2,1,0:T(8,128)} fusion(bf16[2048,2,320]{0,2,1:T(8,128)(2,1)S(1)} %bitcast.134, bf16[320,2,320]{2,1,0:T(2,128)(2,1)S(1)} %get-tuple-element.23), kind=kOutput, calls=%fused_computation.47 | convolution fusion | flops 838860800 | bytes 8273920 | tf_op jit(solution)/shard_map/thd,fhd->thf/dot_general | solution.py:54
  75.4 1.5 fusion.22
  76.9 2.3 copy-done.2
  79.3 1.7 fusion.33
  81.0 7.2 %fusion.25 = f32[320,1,2,320]{3,0,2,1:T(8,128)} fusion(bf16[2048,2,320]{0,2,1:T(8,128)(2,1)S(1)} %bitcast.136, f32[2,320,2048]{2,1,0:T(8,128)S(1)} %fusion.40, f32[2,320,2048]{2,1,0:T(8,128)} %fusion.38, f32[2,320,2048]{2,1,0:T(8,128)} %copy-done.2), kind=kOutput, calls=%fused_computation.38 | convolution fusion | flops 851968000 | bytes 19169280 | tf_op jit(solution)/shard_map/thf,thd->fhd/dot_general | solution.py:63
  88.1 4.3 %fusion.28 = f32[320,1,2,320]{3,0,2,1:T(8,128)S(1)} fusion(f32[2,320,2048]{2,1,0:T(8,128)} %fusion.38, bf16[2048,2,320]{0,2,1:T(8,128)(2,1)S(1)} %bitcast.140, f32[2048,2]{0,1:T(2,128)S(1)} %copy-done.10, f32[2,320,2048]{2,1,0:T(8,128)S(1)} %fusion.40), kind=kOutput, calls=%fused_computation.39 | convolution fusion | flops 850657280 | bytes 13942784 | tf_op jit(solution)/shard_map/thf,thd->fhd/dot_general | solution.py:65
  92.4 1.8 pad_maximum_fusion
  94.3 3.2 %copy.55 = bf16[2048,640]{0,1:T(8,128)(2,1)S(1)} copy(bf16[2048,640]{1,0:T(8,128)(2,1)} %param.10) | data formatting | bytes 5242880 | tf_op args[2]
  98.4 2.3 copy_bitcast_fusion
  100.7 149.8 %all-reduce.2.cloned.1.call-done = f32[320,3,2,320]{3,0,2,1:T(8,128)} async-done(((f32[320,3,2,320]{3,0,2,1:T(8,128)}), f32[320,3,2,320]{3,0,2,1:T(8,128)}) %all-reduce.2.cloned.1.call-update) | async-done | bytes 2457616 | tf_op jit(solution)/shard_map/psum | solution.py:66
  250.5 3.1 %fusion.14 = (f32[3,2,320]{2,1,0:T(2,128)S(1)}, f32[3,2,320]{2,1,0:T(2,128)S(1)}) fusion(bf16[320,1,2,320]{3,0,2,1:T(8,128)(2,1)} %get-tuple-element.30, bf16[320,1,2,320]{3,0,2,1:T(8,128)(2,1)} %get-tuple-element.31, bf16[320,1,2,320]{3,0,2,1:T(8,128)(2,1)} %bitcast.142, f32[320,3,2,320]{3,0,2,1:T(8,128)} %all-reduce.2.cloned.1.call-done), kind=kLoop, calls=%fused_computation.28 | loop fusion | flops 4911360 | bytes 3701760 | tf_op jit(solution)/shard_map/reduce_sum | solution.py:69
  255.4 3.9 %fusion.36 = f32[2,320,2048]{2,1,0:T(8,128)} fusion(bf16[2048,2,320]{0,2,1:T(8,128)(2,1)S(1)} %bitcast.137, bf16[320,3,2,320]{3,0,2,1:T(8,128)(2,1)S(1)} %multiply_convert_fusion.1), kind=kOutput, calls=%fused_computation.43 | convolution fusion | flops 838860800 | bytes 8355840 | tf_op jit(solution)/shard_map/thd,fhd->thf/dot_general | solution.py:77
  259.3 8.4 %multiply_reduce_fusion = (f32[2048]{0:T(1024)S(1)}, f32[2,320,2048]{2,1,0:T(8,128)}) fusion(f32[2,320,2048]{2,1,0:T(8,128)} %fusion.36, bf16[2048,2,320]{0,2,1:T(8,128)(2,1)S(1)} %bitcast.138, bf16[320,3,2,320]{3,0,2,1:T(8,128)(2,1)} %copy-done.8), kind=kOutput, calls=%fused_computation.25 | convolution fusion | flops 1688205312 | bytes 14098432 | tf_op jit(solution)/shard_map/thf,fhd->thd/dot_general | solution.py:80
  268.4 4.3 %all-to-all-start.1 = ((f32[8,1,2048]{2,1,0:T(1,128)}), f32[8,1,2048]{2,1,0:T(1,128)S(1)}, u32[]{:S(2)}, u32[]{:S(2)}) async-start(f32[8,1,2048]{2,1,0:T(1,128)} %broadcast_in_dim.5), calls=%async_computation.1 | async-start | bytes 131072 | tf_op jit(solution)/shard_map/all_to_all | solution.py:21
  275.4 2.9 %all-to-all-done.1 = f32[8,1,2048]{2,1,0:T(1,128)S(1)} async-done(((f32[8,1,2048]{2,1,0:T(1,128)}), f32[8,1,2048]{2,1,0:T(1,128)S(1)}, u32[]{:S(2)}, u32[]{:S(2)}) %all-to-all-start.1) | async-done | bytes 65568 | tf_op jit(solution)/shard_map/all_to_all | solution.py:21
  278.4 3.0 %multiply_convert_fusion = bf16[2,320,2048]{2,1,0:T(8,128)(2,1)S(1)} fusion(f32[2,320,2048]{2,1,0:T(8,128)} %get-tuple-element.29, f32[2,320]{1,0:T(2,128)S(1)} %mul.103, f32[2048]{0:T(1024)S(1)} %add_rsqrt_fusion), kind=kLoop, calls=%fused_computation.24 | loop fusion | flops 3932160 | bytes 7875072 | tf_op jit(solution)/shard_map/convert_element_type | solution.py:84
  281.4 2.6 copy.58
  (37 shorter events, 7.0 us)
Async XLA Ops:
  9.4 56.4 %all-to-all-start = ((bf16[32,10,6,320]{3,2,1,0:T(8,128)(2,1)}), bf16[32,10,6,320]{3,2,1,0:T(8,128)(2,1)}, u32[]{:S(2)}, u32[]{:S(2)}) async-start(bf16[32,10,6,320]{3,2,1,0:T(8,128)(2,1)} %broadcast_in_dim.4), calls=%async_computation | async-start | bytes 3932160 | tf_op jit(solution)/shard_map/all_to_all | solution.py:21
  21.1 229.4 %all-reduce.2.cloned.1.call-start = ((), (), s32[]{:S(2)}) async-start(), calls=%async_computation.2 | async-start | bytes 5898240 | tf_op jit(solution)/shard_map/psum | solution.py:66
  70.0 1.5 copy-start.4
  70.0 5.4 %copy-start.3 = (bf16[320,2,320]{2,1,0:T(2,128)(2,1)}, bf16[320,2,320]{2,1,0:T(2,128)(2,1)S(1)}, u32[]{:S(2)}) copy-start(bf16[320,2,320]{2,1,0:T(2,128)(2,1)S(1)} %get-tuple-element.22) | copy-start | bytes 1228804
  71.5 3.9 %copy-start.1 = (bf16[2048,640]{0,1:T(8,128)(2,1)S(1)}, bf16[2048,640]{0,1:T(8,128)(2,1)}, u32[]{:S(2)}) copy-start(bf16[2048,640]{0,1:T(8,128)(2,1)} %copy.52) | copy-start | bytes 7864324
  71.5 3.8 %copy-start.10 = (f32[2048,2]{0,1:T(2,128)S(1)}, f32[2048,2]{0,1:T(2,128)}, u32[]{:S(2)}) copy-start(f32[2048,2]{0,1:T(2,128)} %param.11) | copy-start | bytes 49156
  76.9 2.3 copy-start.2
  88.1 4.3 %copy-start.9 = (f32[320,1,2,320]{3,0,2,1:T(8,128)S(1)}, f32[320,1,2,320]{3,0,2,1:T(8,128)}, u32[]{:S(2)}) copy-start(f32[320,1,2,320]{3,0,2,1:T(8,128)} %fusion.25) | copy-start | bytes 2457604
  94.3 3.2 %copy-start.11 = (f32[640]{0:T(1024)S(1)}, f32[640]{0:T(1024)}, u32[]{:S(2)}) copy-start(f32[640]{0:T(1024)} %param.15) | copy-start | bytes 7684
  98.4 155.2 %copy-start.5 = (bf16[320,2,320]{2,0,1:T(8,128)(2,1)S(1)}, bf16[320,2,320]{2,0,1:T(8,128)(2,1)}, u32[]{:S(2)}) copy-start(bf16[320,2,320]{2,0,1:T(8,128)(2,1)} %copy.77) | copy-start | bytes 1228804
  250.5 3.2 %copy-start = (f32[320,3,2,320]{3,0,2,1:T(8,128)S(1)}, f32[320,3,2,320]{3,0,2,1:T(8,128)}, u32[]{:S(2)}) copy-start(f32[320,3,2,320]{3,0,2,1:T(8,128)} %all-reduce.2.cloned.1.call-done) | copy-start | bytes 7372804
  250.5 3.2 %copy-start.6 = (bf16[320,1,2,320]{3,0,2,1:T(8,128)(2,1)S(1)}, bf16[320,1,2,320]{3,0,2,1:T(8,128)(2,1)}, u32[]{:S(2)}) copy-start(bf16[320,1,2,320]{3,0,2,1:T(8,128)(2,1)} %get-tuple-element.30) | copy-start | bytes 1228804
  250.5 3.4 %copy-start.7 = (bf16[320,1,2,320]{3,0,2,1:T(8,128)(2,1)S(1)}, bf16[320,1,2,320]{3,0,2,1:T(8,128)(2,1)}, u32[]{:S(2)}) copy-start(bf16[320,1,2,320]{3,0,2,1:T(8,128)(2,1)} %get-tuple-element.31) | copy-start | bytes 1228804
  254.3 1.1 copy-start.8
  268.4 9.9 %all-to-all-start.1 = ((f32[8,1,2048]{2,1,0:T(1,128)}), f32[8,1,2048]{2,1,0:T(1,128)S(1)}, u32[]{:S(2)}, u32[]{:S(2)}) async-start(f32[8,1,2048]{2,1,0:T(1,128)} %broadcast_in_dim.5), calls=%async_computation.1 | async-start | bytes 131072 | tf_op jit(solution)/shard_map/all_to_all | solution.py:21
Sparse Core Ops, SparseCore 0:
  94.4 156.0 all-reduce.1
where the time goes:
time: 293 us; the launch traced here: 291 us
  waiting for transfers between devices  190 us (65%)
  matrix products  32.3 us (11%)
  local copies, waits for them, and re-layouts  28.9 us (10%)
  starting transfers between devices  16 us (5%)
  between operations  14.2 us (5%)
  other arithmetic  9.31 us (3%)
    psum x1, waiting for transfers between devices, per_device(): total = lax.psum(jnp.stack([grad_gate, grad_up, grad_down], axis=1), 'ctx')  150 us
    all_to_all x2, waiting for transfers between devices, from_everyone(): lax.all_to_all(jnp.broadcast_to(array[None], (peers, *array.shape)), axis...  40.3 us
    unnamed x32, local copies, waits for them, and re-layouts  19.5 us
    all_to_all x2, starting transfers between devices, from_everyone(): lax.all_to_all(jnp.broadcast_to(array[None], (peers, *array.shape)), axis...  16 us
    dot_general x1, matrix products, per_device(): jnp.einsum('thf,fhd->thd', mixed, new_down, preferred_element_type=jnp.fl...  8.44 us
    dot_general x1, matrix products, per_device(): jnp.einsum('thf,thd->fhd', dgate, keyh, preferred_element_type=jnp.float32)  7.15 us
  transfers between devices with their start and end apart: 3, of which 3 were waited for; matrix products, arithmetic and copies ran while one was open for 6% of the time, Pallas kernels for 0%

commit v1 on v0

v1 whole, which is shorter than its diff:
```python
import jax
import jax.numpy as jnp
from jax import lax
from jax.experimental import pallas as pl
from jax.experimental.pallas import tpu as pltpu
from jax.sharding import Mesh
from jax.sharding import PartitionSpec as P

EPS = 1e-06
X, Z, Y, CORE = 4, 8, 4, 2
DH, FF, HEADS = 320, 320, 16
LOCAL = FF // (X * Z)
BLOCK = FF // X
WIN = 384
LANES = 2 * DH
F32, BF16 = jnp.float32, jnp.bfloat16
NT = (((1,), (1,)), ((), ()))


def shifted(array, axis, by):
    n = lax.axis_size(axis)
    return lax.ppermute(array, axis, [(i, (i - by) % n) for i in range(n)])


def gathered_z(rows):
    every = lax.all_to_all(jnp.broadcast_to(rows[None], (Z, *rows.shape)), "z", 0, 0, tiled=True)
    return jnp.moveaxis(every.reshape(Z, 3, LOCAL, LANES), 0, 1).reshape(3, BLOCK, LANES)


def gathered(rows):
    block = gathered_z(rows)
    return [block] + [shifted(block, "x", s) for s in (1, 2, 3)]


def own_lanes(head):
    lane = lax.broadcasted_iota(jnp.int32, (BLOCK, WIN), 1)
    return lane < DH if head == 0 else lane >= WIN - DH


def side_by_side(first, second):
    lane = lax.broadcasted_iota(jnp.int32, (first.shape[0], WIN - 256), 1)
    middle = jnp.where(lane < DH - 256, first[:, 256:], second[:, : WIN - 256])
    return jnp.concatenate([first[:, :256], middle, second[:, WIN - 256 :]], axis=1)


def update_body(k_ref, v_ref, r_ref, *refs):
    w_refs, g_refs, (osq_ref, wgu, wd, agu, ad) = refs[:X], refs[X : 2 * X], refs[2 * X :]
    step = pl.program_id(0)

    @pl.when(step == 0)
    def _():
        sq = [jnp.zeros((1, LANES), F32) for _ in range(3)]
        for b, w_ref in enumerate(w_refs):
            for m in range(3):
                w = w_ref[m]
                wf = w.astype(F32)
                sq[m] += jnp.sum(wf * wf, axis=0, keepdims=True)
                for h in range(2):
                    part = jnp.where(own_lanes(h), w[:, h * 256 : h * 256 + WIN], jnp.zeros((), BF16))
                    if m < 2:
                        wgu[h, pl.ds(m * FF + b * BLOCK, BLOCK), :] = part
                    else:
                        wd[h, pl.ds(b * BLOCK, BLOCK), :] = part
        for m in range(3):
            osq_ref[m : m + 1, :] = sq[m]
        agu[...] = jnp.zeros_like(agu)
        ad[...] = jnp.zeros_like(ad)

    for h in range(2):
        k = k_ref[:, h * 256 : h * 256 + WIN]
        v = v_ref[:, h * 256 : h * 256 + WIN]
        rate = r_ref[h : h + 1, :]
        gu = lax.dot_general(wgu[h], k, NT, preferred_element_type=F32)
        back = lax.dot_general(wd[h], v, NT, preferred_element_type=F32) * rate
        g, u = gu[:FF], gu[FF:]
        s = 0.5 * jnp.tanh(0.5 * g) + 0.5
        act = g * s
        slope = s + act * (1.0 - s)
        dgate = (back * u * slope).astype(BF16)
        dup = (back * act).astype(BF16)
        hidden = (act * u * rate).astype(BF16)
        agu[h] += jnp.dot(jnp.concatenate([dgate, dup], axis=0), k, preferred_element_type=F32)
        ad[h] += jnp.dot(hidden, v, preferred_element_type=F32)

    @pl.when(step == pl.num_programs(0) - 1)
    def _():
        for b, g_ref in enumerate(g_refs):
            for m in range(3):
                acc, at = (agu, m * FF + b * BLOCK) if m < 2 else (ad, b * BLOCK)
                rows = pl.ds(at, BLOCK)
                g_ref[m] = side_by_side(acc[0, rows, :], acc[1, rows, :]).astype(BF16)


def update(keys, values, rates, blocks, tile=512):
    tokens = keys.shape[0]
    whole = pl.BlockSpec((3, BLOCK, LANES), lambda i: (0, 0, 0))
    rowspec = pl.BlockSpec((tile, LANES), lambda i: (i, 0))
    outs = pl.pallas_call(
        update_body,
        grid=(tokens // tile,),
        in_specs=[rowspec, rowspec, pl.BlockSpec((2, tile), lambda i: (0, i))] + [whole] * X,
        out_specs=[whole] * X + [pl.BlockSpec((3, LANES), lambda i: (0, 0))],
        out_shape=[jax.ShapeDtypeStruct((3, BLOCK, LANES), BF16)] * X + [jax.ShapeDtypeStruct((3, LANES), F32)],
        scratch_shapes=[
            pltpu.VMEM((2, 2 * FF, WIN), BF16),
            pltpu.VMEM((2, FF, WIN), BF16),
            pltpu.VMEM((2, 2 * FF, WIN), F32),
            pltpu.VMEM((2, FF, WIN), F32),
        ],
        cost_estimate=pl.CostEstimate(
            flops=24 * tokens * FF * WIN, bytes_accessed=4 * tokens * LANES, transcendentals=2 * tokens * FF
        ),
        name="update",
    )(keys, values, rates, *blocks)
    return outs[:X], outs[X]


def apply_body(q_ref, osq_ref, *refs):
    u_refs, (o_ref, sq_ref, sc_ref, wgu, wd) = refs[:X], refs[X:]

    @pl.when(pl.program_id(0) == 0)
    def _():
        wgu[...] = jnp.zeros_like(wgu)
        wd[...] = jnp.zeros_like(wd)
        for m in range(3):
            sq = jnp.zeros((1, LANES), F32)
            for u_ref in u_refs:
                wf = u_ref[m].astype(F32)
                sq += jnp.sum(wf * wf, axis=0, keepdims=True)
            sc = jnp.sqrt(osq_ref[m : m + 1, :]) * lax.rsqrt(sq + EPS)
            sc_ref[m : m + 1, :] = sc
            for b, u_ref in enumerate(u_refs):
                for h in range(2):
                    cols = slice(h * 256, h * 256 + WIN)
                    if m < 2:
                        part = (u_ref[m, :, cols].astype(F32) * sc[:, cols]).astype(BF16)
                        part = jnp.where(own_lanes(h), part, jnp.zeros((), BF16))
                        wgu[h, pl.ds(m * WIN + b * BLOCK, BLOCK), :] = part
                    else:
                        wd[h, pl.ds(b * BLOCK, BLOCK), :] = u_ref[m, :, cols]

    outs = []
    for h in range(2):
        q = q_ref[:, h * 256 : h * 256 + WIN]
        gu = lax.dot_general(q, wgu[h], NT, preferred_element_type=F32)
        g, u = gu[:, :WIN], gu[:, WIN:]
        mixed = (g * (0.5 * jnp.tanh(0.5 * g) + 0.5) * u).astype(BF16)
        outs.append(jnp.dot(mixed, wd[h], preferred_element_type=F32))
    o = side_by_side(*outs) * sc_ref[2:3, :]
    o_ref[...] = o
    ones = jnp.ones((8, LANES), F32)
    sq_ref[...] = lax.dot_general(ones, o * o, NT, preferred_element_type=F32)[:1]


def apply(queries, old_sq, blocks, tile=512):
    tokens = queries.shape[0]
    whole = pl.BlockSpec((3, BLOCK, LANES), lambda i: (0, 0, 0))
    small = pl.BlockSpec((3, LANES), lambda i: (0, 0))
    return pl.pallas_call(
        apply_body,
        grid=(tokens // tile,),
        in_specs=[pl.BlockSpec((tile, LANES), lambda i: (i, 0)), small] + [whole] * X,
        out_specs=[
            pl.BlockSpec((tile, LANES), lambda i: (i, 0)),
            pl.BlockSpec((1, tile), lambda i: (0, i)),
            small,
        ],
        out_shape=[
            jax.ShapeDtypeStruct((tokens, LANES), F32),
            jax.ShapeDtypeStruct((1, tokens), F32),
            jax.ShapeDtypeStruct((3, LANES), F32),
        ],
        scratch_shapes=[pltpu.VMEM((2, 2 * WIN, WIN), BF16), pltpu.VMEM((2, WIN, WIN), BF16)],
        cost_estimate=pl.CostEstimate(
            flops=12 * tokens * FF * WIN, bytes_accessed=6 * tokens * LANES, transcendentals=2 * tokens * FF
        ),
        name="apply",
    )(queries, old_sq, *blocks)


def scale_body(o_ref, sq_ref, gain_ref, out_ref):
    gain = gain_ref[...]
    for j in range(o_ref.shape[0] // 128):
        rows = pl.ds(j * 128, 128)
        scale = lax.rsqrt(sq_ref[:, rows] / (HEADS * DH) + EPS)
        across = jnp.transpose(jnp.broadcast_to(scale, (128, 128)))
        for c in range(LANES // 128):
            cols = slice(c * 128, (c + 1) * 128)
            out_ref[rows, cols] = (o_ref[rows, cols] * across * gain[:, cols]).astype(BF16)


def scaled_output(o, squares, gain, tile=512):
    tokens = o.shape[0]
    rowspec = pl.BlockSpec((tile, LANES), lambda i: (i, 0))
    return pl.pallas_call(
        scale_body,
        grid=(tokens // tile,),
        in_specs=[rowspec, pl.BlockSpec((1, tile), lambda i: (0, i)), pl.BlockSpec((1, LANES), lambda i: (0, 0))],
        out_specs=rowspec,
        out_shape=jax.ShapeDtypeStruct((tokens, LANES), BF16),
        name="scale",
    )(o, squares, gain)


def per_device(keys, values, queries, rates, w_gate, w_up, w_down, gain):
    own = jnp.stack([w.reshape(LOCAL, LANES) for w in (w_gate, w_up, w_down)]).reshape(3 * LOCAL, LANES)
    grads, old_sq = update(keys, values, rates.T, gathered(own))

    total = grads[0].astype(F32)
    for s in (1, 2, 3):
        total += shifted(grads[s], "x", -s).astype(F32)
    pieces = jnp.moveaxis(total.astype(BF16).reshape(3, Z, LOCAL, LANES), 1, 0).reshape(Z, 3 * LOCAL, LANES)
    pieces = lax.all_to_all(pieces, "z", 0, 0, tiled=True)
    updated = own.astype(F32) + jnp.sum(pieces.astype(F32), axis=0)

    o, squares, scale = apply(queries, old_sq, gathered(updated.astype(BF16)))
    squares += shifted(squares, "core", 1)
    squares = squares + shifted(squares, "y", 1) + shifted(squares, "y", 2) + shifted(squares, "y", 3)
    output = scaled_output(o, squares, gain.reshape(1, LANES))
    fresh = (updated.reshape(3, LOCAL, LANES) * scale[:, None, :]).astype(BF16).reshape(3, LOCAL, 2, DH)
    return output, fresh[0], fresh[1], fresh[2]


def solution(mesh):
    split = Mesh(mesh.devices.reshape(X, Z, Y, CORE), ("x", "z", "y", "core"))
    ctx, head = ("x", "z"), ("y", "core")
    weight = P(ctx, head, None)
    return jax.shard_map(
        per_device,
        mesh=split,
        in_specs=(P(ctx, head),) * 4 + (weight,) * 3 + (P(head),),
        out_specs=(P(ctx, head),) + (weight,) * 3,
        check_vma=False,
    )
```

time: 293 us -> 150 us (0.51)
  waiting for transfers between devices: 190 us -> 32.6 us
  blocking collectives: 0 us -> 53.5 us
  matrix products: 32.3 us -> 0 us
  Pallas kernels: 0 us -> 29.8 us
  local copies, waits for them, and re-layouts: 28.9 us -> 7.44 us
  between operations: 14.2 us -> 0.82 us
  other arithmetic: 9.31 us -> 3.24 us
  starting transfers between devices: 16 us -> 20.4 us
    psum x1 -> x0, waiting for transfers between devices: 150 us -> none  [per_device(): total = lax.psum(jnp.stack([grad_gate, grad_up, grad_down], axis=1), 'ctx')]
    all_to_all x0 -> x3, blocking collectives: none -> 53.5 us  [the longest x2 36.5 us: gathered_z(): lax.all_to_all(jnp.broadcast_to(rows[None], (Z, *rows.shape)), 'z', 0, 0,...]
    all_to_all x2 -> x0, waiting for transfers between devices: 40.3 us -> none  [from_everyone(): lax.all_to_all(jnp.broadcast_to(array[None], (peers, *array.shape)), axis...]
    ppermute x0 -> x13, waiting for transfers between devices: none -> 32.6 us  [shifted(): return lax.ppermute(array, axis, [(i, (i - by) % n) for i in range(n)])]
    dot_general x8 -> x0, matrix products: 32.3 us -> none  [the longest x1 8.44 us: per_device(): jnp.einsum('thf,fhd->thd', mixed, new_down, preferred_element_type=jnp.fl...]
    pallas_call x0 -> x3, Pallas kernels: none -> 29.8 us  [the longest x1 13.7 us: update(): pl.pallas_call(update_body, grid=(tokens // tile,), in_specs=[rowspec, ro...]
    ppermute x0 -> x13, starting transfers between devices: none -> 20.4 us  [shifted(): return lax.ppermute(array, axis, [(i, (i - by) % n) for i in range(n)])]
    unnamed x32 -> x20, local copies, waits for them, and re-layouts: 19.5 us -> 1.47 us
  transfers between devices with their start and end apart: 3 -> 13, of which waited for: 3 -> 11; matrix products, arithmetic and copies ran while one was open for 6% -> 2% of each run, Pallas kernels for 0% -> 0%
where the time goes in v1:
time: 150 us; the launch traced here: 148 us
  blocking collectives  53.5 us (36%)
  waiting for transfers between devices  32.6 us (22%)
  Pallas kernels  29.8 us (20%)
  starting transfers between devices  20.4 us (14%)
  local copies, waits for them, and re-layouts  7.44 us (5%)
  other arithmetic  3.24 us (2%)
    all_to_all x2, blocking collectives, gathered_z(): lax.all_to_all(jnp.broadcast_to(rows[None], (Z, *rows.shape)), 'z', 0, 0,...  36.5 us
    ppermute x13, waiting for transfers between devices, shifted(): return lax.ppermute(array, axis, [(i, (i - by) % n) for i in range(n)])  32.6 us
    ppermute x13, starting transfers between devices, shifted(): return lax.ppermute(array, axis, [(i, (i - by) % n) for i in range(n)])  20.4 us
    all_to_all x1, blocking collectives, per_device(): pieces = lax.all_to_all(pieces, 'z', 0, 0, tiled=True)  17 us
    pallas_call x1, Pallas kernels, update(): pl.pallas_call(update_body, grid=(tokens // tile,), in_specs=[rowspec, ro...  13.7 us
    pallas_call x1, Pallas kernels, apply(): pl.pallas_call(apply_body, grid=(tokens // tile,), in_specs=[pl.BlockSpec...  11.3 us
    pallas_call x1, Pallas kernels, scaled_output(): pl.pallas_call(scale_body, grid=(tokens // tile,), in_specs=[rowspec, pl....  4.89 us
  transfers between devices with their start and end apart: 13, of which 11 were waited for; matrix products, arithmetic and copies ran while one was open for 2% of the time, Pallas kernels for 0%

profile of v1, /device:TPU:2, one launch (start us, length us, event | category | flops | bytes accessed | tf_op | source)
XLA Modules:
  0.0 147.8 jit_solution(15116569256215376072)
XLA Ops:
  3.2 21.5 %all_to_all.15 = bf16[8,30,640]{2,1,0:T(8,128)(2,1)S(1)} all-to-all(bf16[8,30,640]{2,1,0:T(8,128)(2,1)S(1)} %broadcast_in_dim.7), channel_id=1, replica_groups=mesh['x'=4,'z'=8,'y'=4,'core'=2] {'z'}, dimensions={0} | all-to-all | bytes 614400 | tf_op jit(solution)/shard_map/all_to_all | solution.py:26
  25.0 1.6 %collective-permute-start.2 = (bf16[3,80,640]{2,1,0:T(8,128)(2,1)S(1)}, bf16[3,80,640]{2,1,0:T(8,128)(2,1)S(1)}, u32[]{:S(2)}, u32[]{:S(2)}) collective-permute-start(bf16[3,80,640]{2,1,0:T(8,128)(2,1)S(1)} %reshape.51.refs_0_), channel_id=1, source_target_pairs={{0,64},{64,128},{128,192},{192,0},{1,65},{65,129},{129,193},{193,1... | collective-permute-start | bytes 921608 | tf_op jit(solution)/shard_map/ppermute | solution.py:22
  27.7 2.2 %collective-permute-start = (bf16[3,80,640]{2,1,0:T(8,128)(2,1)S(1)}, bf16[3,80,640]{2,1,0:T(8,128)(2,1)S(1)}, u32[]{:S(2)}, u32[]{:S(2)}) collective-permute-start(bf16[3,80,640]{2,1,0:T(8,128)(2,1)S(1)} %reshape.51.refs_0_), channel_id=1, source_target_pairs={{0,192},{64,0},{128,64},{192,128},{1,193},{65,1},{129,65},{193,129... | collective-permute-start | bytes 921608 | tf_op jit(solution)/shard_map/ppermute | solution.py:22
  29.8 5.5 %collective-permute-done.2.refs_3_ = bf16[3,80,640]{2,1,0:T(8,128)(2,1)S(1)} collective-permute-done((bf16[3,80,640]{2,1,0:T(8,128)(2,1)S(1)}, bf16[3,80,640]{2,1,0:T(8,128)(2,1)S(1)}, u32[]{:S(2)}, u32[]{:S(2)}) %collective-permute-start.2) | collective-permute-done | bytes 307232 | tf_op jit(solution)/shard_map/ppermute | solution.py:22
  35.3 3.0 %collective-permute-done.1.refs_2_ = bf16[3,80,640]{2,1,0:T(8,128)(2,1)S(1)} collective-permute-done((bf16[3,80,640]{2,1,0:T(8,128)(2,1)S(1)}, bf16[3,80,640]{2,1,0:T(8,128)(2,1)S(1)}, u32[]{:S(2)}, u32[]{:S(2)}) %collective-permute-start.1) | collective-permute-done | bytes 307232 | tf_op jit(solution)/shard_map/ppermute | solution.py:22
  38.3 2.6 %collective-permute-done.refs_1_ = bf16[3,80,640]{2,1,0:T(8,128)(2,1)S(1)} collective-permute-done((bf16[3,80,640]{2,1,0:T(8,128)(2,1)S(1)}, bf16[3,80,640]{2,1,0:T(8,128)(2,1)S(1)}, u32[]{:S(2)}, u32[]{:S(2)}) %collective-permute-start) | collective-permute-done | bytes 307232 | tf_op jit(solution)/shard_map/ppermute | solution.py:22
  41.6 13.7 %update.1 = (bf16[3,80,640]{2,1,0:T(8,128)(2,1)}, bf16[3,80,640]{2,1,0:T(8,128)(2,1)}, bf16[3,80,640]{2,1,0:T(8,128)(2,1)}, bf16[3,80,640]{2,1,0:T(8,128)(2,1)}, f32[3,640]{1,0:T(4,128)}) custom-call(bf16[2048,640]{1,0:T(8,128)(2,1)} %k_ref.1, bf16[2048,640]{1,0:T(8,128)(2,1)} %v_ref.1, f32[2,2048]{1,0:T(2,128)} %bitcast.13, bf16[3,80,640]{2,1,0:T(8,128)(2,1)} %copy-done.1, ...), custom_call_target="tpu_custom_call" | custom-call | flops 6039797760 | bytes 5242880 | tf_op jit(solution)/shard_map/update/pallas_call | solution.py:98
  56.5 1.6 %collective-permute-start.4 = (bf16[3,80,640]{2,1,0:T(8,128)(2,1)}, bf16[3,80,640]{2,1,0:T(8,128)(2,1)S(1)}, u32[]{:S(2)}, u32[]{:S(2)}) collective-permute-start(bf16[3,80,640]{2,1,0:T(8,128)(2,1)} %get-tuple-element.15), channel_id=1, source_target_pairs={{0,128},{64,192},{128,0},{192,64},{1,129},{65,193},{129,1},{193,65... | collective-permute-start | bytes 921608 | tf_op jit(solution)/shard_map/ppermute | solution.py:22
  58.1 1.6 %collective-permute-start.5 = (bf16[3,80,640]{2,1,0:T(8,128)(2,1)}, bf16[3,80,640]{2,1,0:T(8,128)(2,1)S(1)}, u32[]{:S(2)}, u32[]{:S(2)}) collective-permute-start(bf16[3,80,640]{2,1,0:T(8,128)(2,1)} %get-tuple-element.16), channel_id=1, source_target_pairs={{0,192},{64,0},{128,64},{192,128},{1,193},{65,1},{129,65},{193,129... | collective-permute-start | bytes 921608 | tf_op jit(solution)/shard_map/ppermute | solution.py:22
  59.7 6.0 %collective-permute-done.3 = bf16[3,80,640]{2,1,0:T(8,128)(2,1)S(1)} collective-permute-done((bf16[3,80,640]{2,1,0:T(8,128)(2,1)}, bf16[3,80,640]{2,1,0:T(8,128)(2,1)S(1)}, u32[]{:S(2)}, u32[]{:S(2)}) %collective-permute-start.3) | collective-permute-done | bytes 307232 | tf_op jit(solution)/shard_map/ppermute | solution.py:22
  65.7 2.8 %collective-permute-done.4 = bf16[3,80,640]{2,1,0:T(8,128)(2,1)S(1)} collective-permute-done((bf16[3,80,640]{2,1,0:T(8,128)(2,1)}, bf16[3,80,640]{2,1,0:T(8,128)(2,1)S(1)}, u32[]{:S(2)}, u32[]{:S(2)}) %collective-permute-start.4) | collective-permute-done | bytes 307232 | tf_op jit(solution)/shard_map/ppermute | solution.py:22
  68.5 3.3 %collective-permute-done.5 = bf16[3,80,640]{2,1,0:T(8,128)(2,1)S(1)} collective-permute-done((bf16[3,80,640]{2,1,0:T(8,128)(2,1)}, bf16[3,80,640]{2,1,0:T(8,128)(2,1)S(1)}, u32[]{:S(2)}, u32[]{:S(2)}) %collective-permute-start.5) | collective-permute-done | bytes 307232 | tf_op jit(solution)/shard_map/ppermute | solution.py:22
  73.2 17.0 %all_to_all.16 = bf16[8,30,640]{2,1,0:T(8,128)(2,1)S(1)} all-to-all(bf16[8,30,640]{2,1,0:T(8,128)(2,1)S(1)} %copy.18), channel_id=1, replica_groups=mesh['x'=4,'z'=8,'y'=4,'core'=2] {'z'}, dimensions={0} | all-to-all | bytes 614400 | tf_op jit(solution)/shard_map/all_to_all | solution.py:213
  90.3 15.0 %all_to_all.17 = bf16[8,30,640]{2,1,0:T(8,128)(2,1)S(1)} all-to-all(bf16[8,30,640]{2,1,0:T(8,128)(2,1)S(1)} %broadcast_in_dim.16), channel_id=1, replica_groups=mesh['x'=4,'z'=8,'y'=4,'core'=2] {'z'}, dimensions={0} | all-to-all | bytes 614400 | tf_op jit(solution)/shard_map/all_to_all | solution.py:26
  105.6 2.5 %collective-permute-start.7 = (bf16[3,80,640]{2,1,0:T(8,128)(2,1)S(1)}, bf16[3,80,640]{2,1,0:T(8,128)(2,1)S(1)}, u32[]{:S(2)}, u32[]{:S(2)}) collective-permute-start(bf16[3,80,640]{2,1,0:T(8,128)(2,1)S(1)} %reshape.55.refs_0_), channel_id=1, source_target_pairs={{0,128},{64,192},{128,0},{192,64},{1,129},{65,193},{129,1},{193,65... | collective-permute-start | bytes 921608 | tf_op jit(solution)/shard_map/ppermute | solution.py:22
  108.1 2.5 %collective-permute-start.6 = (bf16[3,80,640]{2,1,0:T(8,128)(2,1)S(1)}, bf16[3,80,640]{2,1,0:T(8,128)(2,1)S(1)}, u32[]{:S(2)}, u32[]{:S(2)}) collective-permute-start(bf16[3,80,640]{2,1,0:T(8,128)(2,1)S(1)} %reshape.55.refs_0_), channel_id=1, source_target_pairs={{0,192},{64,0},{128,64},{192,128},{1,193},{65,1},{129,65},{193,129... | collective-permute-start | bytes 921608 | tf_op jit(solution)/shard_map/ppermute | solution.py:22
  111.3 3.8 %collective-permute-done.8.refs_3_ = bf16[3,80,640]{2,1,0:T(8,128)(2,1)S(1)} collective-permute-done((bf16[3,80,640]{2,1,0:T(8,128)(2,1)S(1)}, bf16[3,80,640]{2,1,0:T(8,128)(2,1)S(1)}, u32[]{:S(2)}, u32[]{:S(2)}) %collective-permute-start.8) | collective-permute-done | bytes 307232 | tf_op jit(solution)/shard_map/ppermute | solution.py:22
  115.1 1.8 %collective-permute-done.7.refs_2_ = bf16[3,80,640]{2,1,0:T(8,128)(2,1)S(1)} collective-permute-done((bf16[3,80,640]{2,1,0:T(8,128)(2,1)S(1)}, bf16[3,80,640]{2,1,0:T(8,128)(2,1)S(1)}, u32[]{:S(2)}, u32[]{:S(2)}) %collective-permute-start.7) | collective-permute-done | bytes 307232 | tf_op jit(solution)/shard_map/ppermute | solution.py:22
  116.9 3.1 %collective-permute-done.6.refs_1_ = bf16[3,80,640]{2,1,0:T(8,128)(2,1)S(1)} collective-permute-done((bf16[3,80,640]{2,1,0:T(8,128)(2,1)S(1)}, bf16[3,80,640]{2,1,0:T(8,128)(2,1)S(1)}, u32[]{:S(2)}, u32[]{:S(2)}) %collective-permute-start.6) | collective-permute-done | bytes 307232 | tf_op jit(solution)/shard_map/ppermute | solution.py:22
  120.7 11.3 %apply.1 = (f32[2048,640]{1,0:T(8,128)}, f32[1,2048]{1,0:T(1,128)}, f32[3,640]{1,0:T(4,128)}) custom-call(bf16[2048,640]{1,0:T(8,128)(2,1)} %q_ref.1, f32[3,640]{1,0:T(4,128)} %get-tuple-element.12.osq_ref, bf16[3,80,640]{2,1,0:T(8,128)(2,1)} %copy-done, bf16[3,80,640]{2,1,0:T(8,128)(2,1)} %copy-done.7, bf16[3,80,640]{2,1,0:T(8,128)(2,1)} %copy-done.5, ...), custom_call_target="tpu_custom_call" | custom-call | flops 3019898880 | bytes 7864320 | tf_op jit(solution)/shard_map/apply/pallas_call | solution.py:159
  134.1 1.6 %collective-permute-start.12 = (f32[1,2048]{1,0:T(1,128)S(1)}, f32[1,2048]{1,0:T(1,128)S(1)}, u32[]{:S(2)}, u32[]{:S(2)}) collective-permute-start(f32[1,2048]{1,0:T(1,128)S(1)} %add.35), channel_id=1, source_target_pairs={{0,2},{2,4},{4,6},{6,0},{1,3},{3,5},{5,7},{7,1},{8,10},{10,12},{12... | collective-permute-start | bytes 24584 | tf_op jit(solution)/shard_map/ppermute | solution.py:22
  135.7 2.9 %collective-permute-start.11 = (f32[1,2048]{1,0:T(1,128)S(1)}, f32[1,2048]{1,0:T(1,128)S(1)}, u32[]{:S(2)}, u32[]{:S(2)}) collective-permute-start(f32[1,2048]{1,0:T(1,128)S(1)} %add.35), channel_id=1, source_target_pairs={{0,4},{2,6},{4,0},{6,2},{1,5},{3,7},{5,1},{7,3},{8,12},{10,14},{12... | collective-permute-start | bytes 24584 | tf_op jit(solution)/shard_map/ppermute | solution.py:22
  138.6 1.3 collective-permute-start.10
  142.9 4.9 %scale.1 = bf16[2048,640]{1,0:T(8,128)(2,1)} custom-call(f32[2048,640]{1,0:T(8,128)} %get-tuple-element.17.o_ref, f32[1,2048]{1,0:T(1,128)} %add_add_fusion.sq_ref, f32[1,640]{1,0:T(1,128)} %reshape.56.gain_ref), custom_call_target="tpu_custom_call" | custom-call | tf_op jit(solution)/shard_map/scale/pallas_call | solution.py:195
  (56 shorter events, 14.0 us)
Async XLA Ops:
  25.0 15.8 %copy-start.1 = (bf16[3,80,640]{2,1,0:T(8,128)(2,1)}, bf16[3,80,640]{2,1,0:T(8,128)(2,1)S(1)}, u32[]{:S(2)}) copy-start(bf16[3,80,640]{2,1,0:T(8,128)(2,1)S(1)} %reshape.51.refs_0_) | copy-start | bytes 921604
  25.0 10.3 %collective-permute-start.2 = (bf16[3,80,640]{2,1,0:T(8,128)(2,1)S(1)}, bf16[3,80,640]{2,1,0:T(8,128)(2,1)S(1)}, u32[]{:S(2)}, u32[]{:S(2)}) collective-permute-start(bf16[3,80,640]{2,1,0:T(8,128)(2,1)S(1)} %reshape.51.refs_0_), channel_id=1, source_target_pairs={{0,64},{64,128},{128,192},{192,0},{1,65},{65,129},{129,193},{193,1... | collective-permute-start | bytes 921608 | tf_op jit(solution)/shard_map/ppermute | solution.py:22
  26.6 11.7 %collective-permute-start.1 = (bf16[3,80,640]{2,1,0:T(8,128)(2,1)S(1)}, bf16[3,80,640]{2,1,0:T(8,128)(2,1)S(1)}, u32[]{:S(2)}, u32[]{:S(2)}) collective-permute-start(bf16[3,80,640]{2,1,0:T(8,128)(2,1)S(1)} %reshape.51.refs_0_), channel_id=1, source_target_pairs={{0,128},{64,192},{128,0},{192,64},{1,129},{65,193},{129,1},{193,65... | collective-permute-start | bytes 921608 | tf_op jit(solution)/shard_map/ppermute | solution.py:22
  27.7 13.1 %collective-permute-start = (bf16[3,80,640]{2,1,0:T(8,128)(2,1)S(1)}, bf16[3,80,640]{2,1,0:T(8,128)(2,1)S(1)}, u32[]{:S(2)}, u32[]{:S(2)}) collective-permute-start(bf16[3,80,640]{2,1,0:T(8,128)(2,1)S(1)} %reshape.51.refs_0_), channel_id=1, source_target_pairs={{0,192},{64,0},{128,64},{192,128},{1,193},{65,1},{129,65},{193,129... | collective-permute-start | bytes 921608 | tf_op jit(solution)/shard_map/ppermute | solution.py:22
  35.3 5.5 %copy-start.4 = (bf16[3,80,640]{2,1,0:T(8,128)(2,1)}, bf16[3,80,640]{2,1,0:T(8,128)(2,1)S(1)}, u32[]{:S(2)}) copy-start(bf16[3,80,640]{2,1,0:T(8,128)(2,1)S(1)} %collective-permute-done.2.refs_3_) | copy-start | bytes 921604
  38.3 2.6 %copy-start.6 = (bf16[3,80,640]{2,1,0:T(8,128)(2,1)}, bf16[3,80,640]{2,1,0:T(8,128)(2,1)S(1)}, u32[]{:S(2)}) copy-start(bf16[3,80,640]{2,1,0:T(8,128)(2,1)S(1)} %collective-permute-done.1.refs_2_) | copy-start | bytes 921604
  40.8 0.7 copy-start.8
  55.2 10.4 %collective-permute-start.3 = (bf16[3,80,640]{2,1,0:T(8,128)(2,1)}, bf16[3,80,640]{2,1,0:T(8,128)(2,1)S(1)}, u32[]{:S(2)}, u32[]{:S(2)}) collective-permute-start(bf16[3,80,640]{2,1,0:T(8,128)(2,1)} %get-tuple-element.14), channel_id=1, source_target_pairs={{0,64},{64,128},{128,192},{192,0},{1,65},{65,129},{129,193},{193,1... | collective-permute-start | bytes 921608 | tf_op jit(solution)/shard_map/ppermute | solution.py:22
  56.5 11.9 %collective-permute-start.4 = (bf16[3,80,640]{2,1,0:T(8,128)(2,1)}, bf16[3,80,640]{2,1,0:T(8,128)(2,1)S(1)}, u32[]{:S(2)}, u32[]{:S(2)}) collective-permute-start(bf16[3,80,640]{2,1,0:T(8,128)(2,1)} %get-tuple-element.15), channel_id=1, source_target_pairs={{0,128},{64,192},{128,0},{192,64},{1,129},{65,193},{129,1},{193,65... | collective-permute-start | bytes 921608 | tf_op jit(solution)/shard_map/ppermute | solution.py:22
  58.1 13.7 %collective-permute-start.5 = (bf16[3,80,640]{2,1,0:T(8,128)(2,1)}, bf16[3,80,640]{2,1,0:T(8,128)(2,1)S(1)}, u32[]{:S(2)}, u32[]{:S(2)}) collective-permute-start(bf16[3,80,640]{2,1,0:T(8,128)(2,1)} %get-tuple-element.16), channel_id=1, source_target_pairs={{0,192},{64,0},{128,64},{192,128},{1,193},{65,1},{129,65},{193,129... | collective-permute-start | bytes 921608 | tf_op jit(solution)/shard_map/ppermute | solution.py:22
  73.1 37.6 %copy-start.2 = (f32[640]{0:T(1024)S(1)}, f32[640]{0:T(1024)}, u32[]{:S(2)}) copy-start(f32[640]{0:T(1024)} %param.15) | copy-start | bytes 7684
  105.5 14.5 %copy-start = (bf16[3,80,640]{2,1,0:T(8,128)(2,1)}, bf16[3,80,640]{2,1,0:T(8,128)(2,1)S(1)}, u32[]{:S(2)}) copy-start(bf16[3,80,640]{2,1,0:T(8,128)(2,1)S(1)} %reshape.55.refs_0_) | copy-start | bytes 921604
  105.5 9.6 %collective-permute-start.8 = (bf16[3,80,640]{2,1,0:T(8,128)(2,1)S(1)}, bf16[3,80,640]{2,1,0:T(8,128)(2,1)S(1)}, u32[]{:S(2)}, u32[]{:S(2)}) collective-permute-start(bf16[3,80,640]{2,1,0:T(8,128)(2,1)S(1)} %reshape.55.refs_0_), channel_id=1, source_target_pairs={{0,64},{64,128},{128,192},{192,0},{1,65},{65,129},{129,193},{193,1... | collective-permute-start | bytes 921608 | tf_op jit(solution)/shard_map/ppermute | solution.py:22
  105.6 11.3 %collective-permute-start.7 = (bf16[3,80,640]{2,1,0:T(8,128)(2,1)S(1)}, bf16[3,80,640]{2,1,0:T(8,128)(2,1)S(1)}, u32[]{:S(2)}, u32[]{:S(2)}) collective-permute-start(bf16[3,80,640]{2,1,0:T(8,128)(2,1)S(1)} %reshape.55.refs_0_), channel_id=1, source_target_pairs={{0,128},{64,192},{128,0},{192,64},{1,129},{65,193},{129,1},{193,65... | collective-permute-start | bytes 921608 | tf_op jit(solution)/shard_map/ppermute | solution.py:22
  108.1 11.9 %collective-permute-start.6 = (bf16[3,80,640]{2,1,0:T(8,128)(2,1)S(1)}, bf16[3,80,640]{2,1,0:T(8,128)(2,1)S(1)}, u32[]{:S(2)}, u32[]{:S(2)}) collective-permute-start(bf16[3,80,640]{2,1,0:T(8,128)(2,1)S(1)} %reshape.55.refs_0_), channel_id=1, source_target_pairs={{0,192},{64,0},{128,64},{192,128},{1,193},{65,1},{129,65},{193,129... | collective-permute-start | bytes 921608 | tf_op jit(solution)/shard_map/ppermute | solution.py:22
  115.1 4.9 %copy-start.3 = (bf16[3,80,640]{2,1,0:T(8,128)(2,1)}, bf16[3,80,640]{2,1,0:T(8,128)(2,1)S(1)}, u32[]{:S(2)}) copy-start(bf16[3,80,640]{2,1,0:T(8,128)(2,1)S(1)} %collective-permute-done.8.refs_3_) | copy-start | bytes 921604
  116.9 3.2 %copy-start.5 = (bf16[3,80,640]{2,1,0:T(8,128)(2,1)}, bf16[3,80,640]{2,1,0:T(8,128)(2,1)S(1)}, u32[]{:S(2)}) copy-start(bf16[3,80,640]{2,1,0:T(8,128)(2,1)S(1)} %collective-permute-done.7.refs_2_) | copy-start | bytes 921604
  120.0 0.7 copy-start.7
  132.0 1.4 collective-permute-start.9
  134.1 8.0 %collective-permute-start.12 = (f32[1,2048]{1,0:T(1,128)S(1)}, f32[1,2048]{1,0:T(1,128)S(1)}, u32[]{:S(2)}, u32[]{:S(2)}) collective-permute-start(f32[1,2048]{1,0:T(1,128)S(1)} %add.35), channel_id=1, source_target_pairs={{0,2},{2,4},{4,6},{6,0},{1,3},{3,5},{5,7},{7,1},{8,10},{10,12},{12... | collective-permute-start | bytes 24584 | tf_op jit(solution)/shard_map/ppermute | solution.py:22
  135.7 6.4 %collective-permute-start.11 = (f32[1,2048]{1,0:T(1,128)S(1)}, f32[1,2048]{1,0:T(1,128)S(1)}, u32[]{:S(2)}, u32[]{:S(2)}) collective-permute-start(f32[1,2048]{1,0:T(1,128)S(1)} %add.35), channel_id=1, source_target_pairs={{0,4},{2,6},{4,0},{6,2},{1,5},{3,7},{5,1},{7,3},{8,12},{10,14},{12... | collective-permute-start | bytes 24584 | tf_op jit(solution)/shard_map/ppermute | solution.py:22
  138.6 3.7 %collective-permute-start.10 = (f32[1,2048]{1,0:T(1,128)S(1)}, f32[1,2048]{1,0:T(1,128)S(1)}, u32[]{:S(2)}, u32[]{:S(2)}) collective-permute-start(f32[1,2048]{1,0:T(1,128)S(1)} %add.35), channel_id=1, source_target_pairs={{0,6},{2,0},{4,2},{6,4},{1,7},{3,1},{5,3},{7,5},{8,14},{10,8},{12,... | collective-permute-start | bytes 24584 | tf_op jit(solution)/shard_map/ppermute | solution.py:22

commit v2 on v1

v2 whole, which is shorter than its diff:
```python
import functools

import jax
import jax.numpy as jnp
from jax import lax
from jax.experimental import pallas as pl
from jax.experimental.pallas import tpu as pltpu
from jax.sharding import Mesh
from jax.sharding import PartitionSpec as P

EPS = 1e-06
X, Z, Y, CORE = 4, 8, 4, 2
DH, FF, HEADS = 320, 320, 16
LOCAL = FF // (X * Z)
BLOCK = FF // X
WIN = 384
LANES = 2 * DH
VMEM = 28 << 20
F32, BF16 = jnp.float32, jnp.bfloat16
NT = (((1,), (1,)), ((), ()))


def shifted(array, axis, by):
    n = lax.axis_size(axis)
    return lax.ppermute(array, axis, [(i, (i - by) % n) for i in range(n)])


def gathered_z(copies):
    every = lax.all_to_all(copies, "z", 0, 0, tiled=True)
    return jnp.moveaxis(every.reshape(Z, 3, LOCAL, LANES), 0, 1).reshape(3, BLOCK, LANES)


def in_turn(value, *first):
    return lax.optimization_barrier((value, *first))[0]


def own_lanes(head):
    lane = lax.broadcasted_iota(jnp.int32, (BLOCK, WIN), 1)
    return lane < DH if head == 0 else lane >= WIN - DH


def side_by_side(first, second):
    lane = lax.broadcasted_iota(jnp.int32, (first.shape[0], WIN - 256), 1)
    middle = jnp.where(lane < DH - 256, first[:, 256:], second[:, : WIN - 256])
    return jnp.concatenate([first[:, :256], middle, second[:, WIN - 256 :]], axis=1)


def update_body(blocks, k_ref, v_ref, r_ref, *refs):
    w_refs, g_refs, (osq_ref, wgu, wd, agu, ad) = refs[:blocks], refs[blocks : 2 * blocks], refs[2 * blocks :]
    step = pl.program_id(0)
    units = blocks * BLOCK

    @pl.when(step == 0)
    def _():
        sq = [jnp.zeros((1, LANES), F32) for _ in range(3)]
        for b, w_ref in enumerate(w_refs):
            for m in range(3):
                w = w_ref[m]
                wf = w.astype(F32)
                sq[m] += jnp.sum(wf * wf, axis=0, keepdims=True)
                for h in range(2):
                    part = jnp.where(own_lanes(h), w[:, h * 256 : h * 256 + WIN], jnp.zeros((), BF16))
                    if m < 2:
                        wgu[h, pl.ds(m * units + b * BLOCK, BLOCK), :] = part
                    else:
                        wd[h, pl.ds(b * BLOCK, BLOCK), :] = part
        for m in range(3):
            osq_ref[m : m + 1, :] = sq[m]
        agu[...] = jnp.zeros_like(agu)
        ad[...] = jnp.zeros_like(ad)

    for h in range(2):
        k = k_ref[:, h * 256 : h * 256 + WIN]
        v = v_ref[:, h * 256 : h * 256 + WIN]
        rate = r_ref[h : h + 1, :]
        gu = lax.dot_general(wgu[h], k, NT, preferred_element_type=F32)
        back = lax.dot_general(wd[h], v, NT, preferred_element_type=F32) * rate
        g, u = gu[:units], gu[units:]
        s = 0.5 * jnp.tanh(0.5 * g) + 0.5
        act = g * s
        slope = s + act * (1.0 - s)
        dgate = (back * u * slope).astype(BF16)
        dup = (back * act).astype(BF16)
        hidden = (act * u * rate).astype(BF16)
        agu[h] += jnp.dot(jnp.concatenate([dgate, dup], axis=0), k, preferred_element_type=F32)
        ad[h] += jnp.dot(hidden, v, preferred_element_type=F32)

    @pl.when(step == pl.num_programs(0) - 1)
    def _():
        for b, g_ref in enumerate(g_refs):
            for m in range(3):
                acc, at = (agu, m * units + b * BLOCK) if m < 2 else (ad, b * BLOCK)
                rows = pl.ds(at, BLOCK)
                g_ref[m] = side_by_side(acc[0, rows, :], acc[1, rows, :]).astype(BF16)


def update(keys, values, rates, blocks, tile=1024):
    tokens, n = keys.shape[0], len(blocks)
    whole = pl.BlockSpec((3, BLOCK, LANES), lambda i: (0, 0, 0))
    rowspec = pl.BlockSpec((tile, LANES), lambda i: (i, 0))
    outs = pl.pallas_call(
        functools.partial(update_body, n),
        grid=(tokens // tile,),
        in_specs=[rowspec, rowspec, pl.BlockSpec((2, tile), lambda i: (0, i))] + [whole] * n,
        out_specs=[whole] * n + [pl.BlockSpec((3, LANES), lambda i: (0, 0))],
        out_shape=[jax.ShapeDtypeStruct((3, BLOCK, LANES), BF16)] * n + [jax.ShapeDtypeStruct((3, LANES), F32)],
        scratch_shapes=[
            pltpu.VMEM((2, 2 * n * BLOCK, WIN), BF16),
            pltpu.VMEM((2, n * BLOCK, WIN), BF16),
            pltpu.VMEM((2, 2 * n * BLOCK, WIN), F32),
            pltpu.VMEM((2, n * BLOCK, WIN), F32),
        ],
        cost_estimate=pl.CostEstimate(
            flops=48 * tokens * n * BLOCK * WIN, bytes_accessed=4 * tokens * LANES, transcendentals=2 * tokens * FF
        ),
        compiler_params=pltpu.CompilerParams(vmem_limit_bytes=VMEM),
        name="update",
    )(keys, values, rates, *blocks)
    return outs[:n], outs[n]


def apply_body(part, q_ref, osq_ref, *refs):
    u_refs, (o_ref, sq_ref, sc_ref, wgu, wd) = refs[:X], refs[X:]

    @pl.when(pl.program_id(0) == 0)
    def _():
        wgu[...] = jnp.zeros_like(wgu)
        wd[...] = jnp.zeros_like(wd)
        for m in range(3):
            sq = jnp.zeros((1, LANES), F32)
            for u_ref in u_refs:
                wf = u_ref[m].astype(F32)
                sq += jnp.sum(wf * wf, axis=0, keepdims=True)
            sc = jnp.sqrt(osq_ref[m : m + 1, :]) * lax.rsqrt(sq + EPS)
            sc_ref[m : m + 1, :] = sc
            for b, u_ref in enumerate(u_refs):
                for h in range(2):
                    cols = slice(h * 256, h * 256 + WIN)
                    if m < 2:
                        part = (u_ref[m, :, cols].astype(F32) * sc[:, cols]).astype(BF16)
                        part = jnp.where(own_lanes(h), part, jnp.zeros((), BF16))
                        wgu[h, pl.ds(m * WIN + b * BLOCK, BLOCK), :] = part
                    else:
                        wd[h, pl.ds(b * BLOCK, BLOCK), :] = u_ref[m, :, cols]

    def project(rows, h):
        q = q_ref[rows, h * 256 : h * 256 + WIN]
        return lax.dot_general(q, wgu[h], NT, preferred_element_type=F32)

    def finish(rows, outs):
        o = side_by_side(*outs) * sc_ref[2:3, :]
        o_ref[rows, :] = o
        sq = o * o
        sq = sum(sq[:, c * 128 : (c + 1) * 128] for c in range(1, LANES // 128)) + sq[:, :128]
        for j in range(o.shape[0] // 128):
            at = rows.start // 128 + j
            sq_ref[at : at + 1, :] = jnp.sum(jnp.transpose(sq[j * 128 : (j + 1) * 128]), axis=0, keepdims=True)

    steps = [(slice(r, r + part), h) for r in range(0, q_ref.shape[0], part) for h in range(2)]
    ahead, outs = project(*steps[0]), []
    for i, (rows, h) in enumerate(steps):
        g, u = ahead[:, :WIN], ahead[:, WIN:]
        if i + 1 < len(steps):
            ahead = project(*steps[i + 1])
        mixed = (g * (0.5 * jnp.tanh(0.5 * g) + 0.5) * u).astype(BF16)
        outs.append(jnp.dot(mixed, wd[h], preferred_element_type=F32))
        if h == 1:
            finish(rows, outs)
            outs = []


def apply(queries, old_sq, blocks, tile=1024, part=512):
    tokens = queries.shape[0]
    whole = pl.BlockSpec((3, BLOCK, LANES), lambda i: (0, 0, 0))
    small = pl.BlockSpec((3, LANES), lambda i: (0, 0))
    return pl.pallas_call(
        functools.partial(apply_body, part),
        grid=(tokens // tile,),
        in_specs=[pl.BlockSpec((tile, LANES), lambda i: (i, 0)), small] + [whole] * X,
        out_specs=[
            pl.BlockSpec((tile, LANES), lambda i: (i, 0)),
            pl.BlockSpec((tile // 128, 128), lambda i: (i, 0)),
            small,
        ],
        out_shape=[
            pltpu.HBM((tokens, LANES), F32),
            jax.ShapeDtypeStruct((tokens // 128, 128), F32),
            jax.ShapeDtypeStruct((3, LANES), F32),
        ],
        scratch_shapes=[pltpu.VMEM((2, 2 * WIN, WIN), BF16), pltpu.VMEM((2, WIN, WIN), BF16)],
        cost_estimate=pl.CostEstimate(
            flops=12 * tokens * FF * WIN, bytes_accessed=6 * tokens * LANES, transcendentals=2 * tokens * FF
        ),
        compiler_params=pltpu.CompilerParams(vmem_limit_bytes=VMEM),
        name="apply",
    )(queries, old_sq, *blocks)


def scale_body(o_ref, gain_ref, *refs):
    sq_refs, out_ref = refs[:-1], refs[-1]
    gain = gain_ref[...]
    sq = sum(r[...] for r in sq_refs[1:]) + sq_refs[0][...]
    scale = lax.rsqrt(sq / (HEADS * DH) + EPS)
    for j in range(o_ref.shape[0] // 128):
        rows = pl.ds(j * 128, 128)
        across = jnp.transpose(jnp.broadcast_to(scale[j : j + 1], (128, 128)))
        for c in range(LANES // 128):
            cols = slice(c * 128, (c + 1) * 128)
            out_ref[rows, cols] = (o_ref[rows, cols] * across * gain[:, cols]).astype(BF16)


def scaled_output(o, squares, gain, tile=1024):
    tokens = o.shape[0]
    rowspec = pl.BlockSpec((tile, LANES), lambda i: (i, 0))
    sqspec = pl.BlockSpec((tile // 128, 128), lambda i: (i, 0))
    return pl.pallas_call(
        scale_body,
        grid=(tokens // tile,),
        in_specs=[rowspec, pl.BlockSpec((1, LANES), lambda i: (0, 0))] + [sqspec] * len(squares),
        out_specs=rowspec,
        out_shape=jax.ShapeDtypeStruct((tokens, LANES), BF16),
        compiler_params=pltpu.CompilerParams(vmem_limit_bytes=VMEM),
        name="scale",
    )(o, gain, *squares)


def pack_body(gate_ref, up_ref, down_ref, own_ref, copies_ref):
    rows = []
    for w_ref in (gate_ref, up_ref, down_ref):
        w = w_ref[...].astype(F32)
        rows.append(jnp.concatenate([w[:, 0, :], w[:, 1, :]], axis=1))
    own = jnp.concatenate(rows, axis=0).astype(BF16)
    own_ref[...] = own
    for z in range(Z):
        copies_ref[z] = own


def packed(weights):
    return pl.pallas_call(
        pack_body,
        out_shape=[
            jax.ShapeDtypeStruct((3 * LOCAL, LANES), BF16),
            jax.ShapeDtypeStruct((Z, 3 * LOCAL, LANES), BF16),
        ],
        name="pack",
    )(*weights)


def per_device(keys, values, queries, rates, w_gate, w_up, w_down, gain):
    own, copies = packed((w_gate, w_up, w_down))
    rates = rates.T
    here = gathered_z(copies)
    across = shifted(here, "x", 2)
    sides = shifted(here, "x", 1), shifted(here, "x", 3)
    (g0,), sq_a = update(keys, values, rates, (here,))
    (g2,), sq_b = update(keys, values, in_turn(rates, g0), (across,))
    r2 = shifted(g2, "x", 2)
    (g1, g3), sq_c = update(keys, values, in_turn(rates, g2), sides)
    r1, r3 = shifted(g1, "x", 3), shifted(g3, "x", 1)
    total = lax.optimization_barrier(g0.astype(F32) + r2.astype(F32)) + r1.astype(F32) + r3.astype(F32)
    old_sq = sq_a + sq_b + sq_c
    pieces = jnp.moveaxis(total.astype(BF16).reshape(3, Z, LOCAL, LANES), 1, 0).reshape(Z, 3 * LOCAL, LANES)
    pieces = lax.all_to_all(pieces, "z", 0, 0, tiled=True)
    updated = own.astype(F32) + jnp.sum(pieces.astype(F32), axis=0)

    here = gathered_z(jnp.broadcast_to(updated.astype(BF16)[None], (Z, 3 * LOCAL, LANES)))
    new = [here] + [shifted(here, "x", s) for s in (1, 3, 2)]
    o, squares, scale = apply(queries, old_sq, new)
    squares = squares.reshape(-1)
    squares += shifted(squares, "core", 1)
    squares = [squares] + [shifted(squares, "y", s) for s in (2, 1, 3)]
    o = pltpu.with_memory_space_constraint(o, pltpu.HBM)
    output = scaled_output(o, [s.reshape(-1, 128) for s in squares], gain.reshape(1, LANES))
    fresh = (updated.reshape(3, LOCAL, LANES) * scale[:, None, :]).astype(BF16).reshape(3, LOCAL, 2, DH)
    return output, fresh[0], fresh[1], fresh[2]


def solution(mesh):
    split = Mesh(mesh.devices.reshape(X, Z, Y, CORE), ("x", "z", "y", "core"))
    ctx, head = ("x", "z"), ("y", "core")
    weight = P(ctx, head, None)
    return jax.shard_map(
        per_device,
        mesh=split,
        in_specs=(P(ctx, head),) * 4 + (weight,) * 3 + (P(head),),
        out_specs=(P(ctx, head),) + (weight,) * 3,
        check_vma=False,
    )
```

time: 150 us -> 122 us (0.81); the launches traced: 148 us -> 122 us
  waiting for transfers between devices: 32.6 us -> 19.1 us
  other arithmetic: 3.24 us -> 0.28 us
  local copies, waits for them, and re-layouts: 7.44 us -> 4.65 us
  starting transfers between devices: 20.4 us -> 17.9 us
  Pallas kernels: 29.8 us -> 27.5 us
  blocking collectives: 53.5 us -> 51.4 us
    ppermute x13, waiting for transfers between devices: 32.6 us -> 19.1 us  [shifted(): return lax.ppermute(array, axis, [(i, (i - by) % n) for i in range(n)])]
    another operation x4 -> x0, local copies, waits for them, and re-layouts: 2.45 us -> none  [per_device(): jnp.stack([w.reshape(LOCAL, LANES) for w in (w_gate, w_up, w_down)])]
    ppermute x13, starting transfers between devices: 20.4 us -> 17.9 us  [shifted(): return lax.ppermute(array, axis, [(i, (i - by) % n) for i in range(n)])]
    pallas_call x2 -> x5, Pallas kernels: 24.9 us -> 23.5 us  [the longest x3 12.9 us: update(): pl.pallas_call(functools.partial(update_body, n), grid=(tokens // tile,),...]
  transfers between devices with their start and end apart: 13 -> 13, of which waited for: 11 -> 8; matrix products, arithmetic and copies ran while one was open for 2% -> 2% of each run, Pallas kernels for 0% -> 11%
where the time goes in v2:
time: 122 us
  blocking collectives  51.4 us (42%)
  Pallas kernels  27.5 us (23%)
  waiting for transfers between devices  19.1 us (16%)
  starting transfers between devices  17.9 us (15%)
  local copies, waits for them, and re-layouts  4.65 us (4%)
    all_to_all x2, blocking collectives, gathered_z(): every = lax.all_to_all(copies, 'z', 0, 0, tiled=True)  35.7 us
    ppermute x13, waiting for transfers between devices, shifted(): return lax.ppermute(array, axis, [(i, (i - by) % n) for i in range(n)])  19.1 us
    ppermute x13, starting transfers between devices, shifted(): return lax.ppermute(array, axis, [(i, (i - by) % n) for i in range(n)])  17.9 us
    all_to_all x1, blocking collectives, per_device(): pieces = lax.all_to_all(pieces, 'z', 0, 0, tiled=True)  15.8 us
    pallas_call x3, Pallas kernels, update(): pl.pallas_call(functools.partial(update_body, n), grid=(tokens // tile,),...  12.9 us
    pallas_call x1, Pallas kernels, apply(): pl.pallas_call(functools.partial(apply_body, part), grid=(tokens // tile,...  8.86 us
    pallas_call x1, Pallas kernels, scaled_output(): pl.pallas_call(scale_body, grid=(tokens // tile,), in_specs=[rowspec, pl....  3.97 us
  transfers between devices with their start and end apart: 13, of which 8 were waited for; matrix products, arithmetic and copies ran while one was open for 2% of the time, Pallas kernels for 11%

profile of v2, /device:TPU:2, one launch (start us, length us, event | category | flops | bytes accessed | tf_op | source)
XLA Modules:
  0.0 121.7 jit_solution(5073477908457024378)
XLA Ops:
  0.7 1.7 %pack.1 = (bf16[30,640]{1,0:T(8,128)(2,1)}, bf16[8,30,640]{2,1,0:T(8,128)(2,1)}) custom-call(bf16[10,2,320]{2,1,0:T(2,128)(2,1)} %gate_ref.1, bf16[10,2,320]{2,1,0:T(2,128)(2,1)} %up_ref.1, bf16[10,2,320]{2,1,0:T(2,128)(2,1)} %down_ref.1), custom_call_target="tpu_custom_call" | custom-call | tf_op jit(solution)/shard_map/pack/pallas_call | solution.py:239
  2.4 21.7 %all_to_all.15 = bf16[8,30,640]{2,1,0:T(8,128)(2,1)S(1)} all-to-all(bf16[8,30,640]{2,1,0:T(8,128)(2,1)} %get-tuple-element.18), channel_id=1, replica_groups=mesh['x'=4,'z'=8,'y'=4,'core'=2] {'z'}, dimensions={0} | all-to-all | bytes 614400 | tf_op jit(solution)/shard_map/all_to_all | solution.py:29
  24.4 2.2 %collective-permute-start = (bf16[3,80,640]{2,1,0:T(8,128)(2,1)S(1)}, bf16[3,80,640]{2,1,0:T(8,128)(2,1)S(1)}, u32[]{:S(2)}, u32[]{:S(2)}) collective-permute-start(bf16[3,80,640]{2,1,0:T(8,128)(2,1)S(1)} %reshape.57.refs_0_), channel_id=1, source_target_pairs={{0,128},{64,192},{128,0},{192,64},{1,129},{65,193},{129,1},{193,65... | collective-permute-start | bytes 921608 | tf_op jit(solution)/shard_map/ppermute | solution.py:25
  26.6 2.0 %collective-permute-start.1 = (bf16[3,80,640]{2,1,0:T(8,128)(2,1)S(1)}, bf16[3,80,640]{2,1,0:T(8,128)(2,1)S(1)}, u32[]{:S(2)}, u32[]{:S(2)}) collective-permute-start(bf16[3,80,640]{2,1,0:T(8,128)(2,1)S(1)} %reshape.57.refs_0_), channel_id=1, source_target_pairs={{0,192},{64,0},{128,64},{192,128},{1,193},{65,1},{129,65},{193,129... | collective-permute-start | bytes 921608 | tf_op jit(solution)/shard_map/ppermute | solution.py:25
  28.7 1.7 %copy-done.1 = bf16[2048,640]{1,0:T(8,128)(2,1)S(1)} copy-done((bf16[2048,640]{1,0:T(8,128)(2,1)S(1)}, bf16[2048,640]{1,0:T(8,128)(2,1)}, u32[]{:S(2)}) %copy-start.1) | copy-done | bytes 2621464
  30.4 3.7 %update.3 = (bf16[3,80,640]{2,1,0:T(8,128)(2,1)S(1)}, f32[3,640]{1,0:T(4,128)S(1)}) custom-call(bf16[2048,640]{1,0:T(8,128)(2,1)S(1)} %copy-done, bf16[2048,640]{1,0:T(8,128)(2,1)S(1)} %copy-done.1, f32[2,2048]{1,0:T(2,128)S(1)} %bitcast.20, bf16[3,80,640]{2,1,0:T(8,128)(2,1)S(1)} %reshape.57.refs_0_), custom_call_target="tpu_custom_call" | custom-call | flops 3019898880 | bytes 5242880 | tf_op jit(solution)/shard_map/update/pallas_call | solution.py:101
  34.1 2.1 %collective-permute-done.refs_0_ = bf16[3,80,640]{2,1,0:T(8,128)(2,1)S(1)} collective-permute-done((bf16[3,80,640]{2,1,0:T(8,128)(2,1)S(1)}, bf16[3,80,640]{2,1,0:T(8,128)(2,1)S(1)}, u32[]{:S(2)}, u32[]{:S(2)}) %collective-permute-start) | collective-permute-done | bytes 307232 | tf_op jit(solution)/shard_map/ppermute | solution.py:25
  36.2 3.7 %update.4 = (bf16[3,80,640]{2,1,0:T(8,128)(2,1)S(1)}, f32[3,640]{1,0:T(4,128)S(1)}) custom-call(bf16[2048,640]{1,0:T(8,128)(2,1)S(1)} %copy-done, bf16[2048,640]{1,0:T(8,128)(2,1)S(1)} %copy-done.1, f32[2,2048]{1,0:T(2,128)S(1)} %bitcast.21, bf16[3,80,640]{2,1,0:T(8,128)(2,1)S(1)} %collective-permute-done.refs_0_), custom_call_target="tpu_custom_call" | custom-call | flops 3019898880 | bytes 5242880 | tf_op jit(solution)/shard_map/update/pallas_call | solution.py:101
  39.9 2.2 %collective-permute-start.3 = (bf16[3,80,640]{2,1,0:T(8,128)(2,1)S(1)}, bf16[3,80,640]{2,1,0:T(8,128)(2,1)S(1)}, u32[]{:S(2)}, u32[]{:S(2)}) collective-permute-start(bf16[3,80,640]{2,1,0:T(8,128)(2,1)S(1)} %get-tuple-element.23), channel_id=1, source_target_pairs={{0,128},{64,192},{128,0},{192,64},{1,129},{65,193},{129,1},{193,65... | collective-permute-start | bytes 921608 | tf_op jit(solution)/shard_map/ppermute | solution.py:25
  42.1 5.6 %update.5 = (bf16[3,80,640]{2,1,0:T(8,128)(2,1)S(1)}, bf16[3,80,640]{2,1,0:T(8,128)(2,1)S(1)}, f32[3,640]{1,0:T(4,128)S(1)}) custom-call(bf16[2048,640]{1,0:T(8,128)(2,1)S(1)} %copy-done, bf16[2048,640]{1,0:T(8,128)(2,1)S(1)} %copy-done.1, f32[2,2048]{1,0:T(2,128)S(1)} %bitcast.22, bf16[3,80,640]{2,1,0:T(8,128)(2,1)S(1)} %collective-permute-done.1.refs_0_, ...), custom_call_target="tpu_custom_call" | custom-call | flops 6039797760 | bytes 5242880 | tf_op jit(solution)/shard_map/update/pallas_call | solution.py:101
  47.8 2.0 %collective-permute-start.5 = (bf16[3,80,640]{2,1,0:T(8,128)(2,1)S(1)}, bf16[3,80,640]{2,1,0:T(8,128)(2,1)S(1)}, u32[]{:S(2)}, u32[]{:S(2)}) collective-permute-start(bf16[3,80,640]{2,1,0:T(8,128)(2,1)S(1)} %get-tuple-element.28), channel_id=1, source_target_pairs={{0,192},{64,0},{128,64},{192,128},{1,193},{65,1},{129,65},{193,129... | collective-permute-start | bytes 921608 | tf_op jit(solution)/shard_map/ppermute | solution.py:25
  49.9 5.1 %collective-permute-done.4 = bf16[3,80,640]{2,1,0:T(8,128)(2,1)S(1)} collective-permute-done((bf16[3,80,640]{2,1,0:T(8,128)(2,1)S(1)}, bf16[3,80,640]{2,1,0:T(8,128)(2,1)S(1)}, u32[]{:S(2)}, u32[]{:S(2)}) %collective-permute-start.4) | collective-permute-done | bytes 307232 | tf_op jit(solution)/shard_map/ppermute | solution.py:25
  55.4 15.8 %all_to_all.16 = bf16[8,30,640]{2,1,0:T(8,128)(2,1)S(1)} all-to-all(bf16[8,30,640]{2,1,0:T(8,128)(2,1)S(1)} %copy.20), channel_id=1, replica_groups=mesh['x'=4,'z'=8,'y'=4,'core'=2] {'z'}, dimensions={0} | all-to-all | bytes 614400 | tf_op jit(solution)/shard_map/all_to_all | solution.py:263
  71.3 13.9 %all_to_all.17 = bf16[8,30,640]{2,1,0:T(8,128)(2,1)S(1)} all-to-all(bf16[8,30,640]{2,1,0:T(8,128)(2,1)S(1)} %broadcast_in_dim.2), channel_id=1, replica_groups=mesh['x'=4,'z'=8,'y'=4,'core'=2] {'z'}, dimensions={0} | all-to-all | bytes 614400 | tf_op jit(solution)/shard_map/all_to_all | solution.py:29
  85.5 2.1 %collective-permute-start.8 = (bf16[3,80,640]{2,1,0:T(8,128)(2,1)S(1)}, bf16[3,80,640]{2,1,0:T(8,128)(2,1)S(1)}, u32[]{:S(2)}, u32[]{:S(2)}) collective-permute-start(bf16[3,80,640]{2,1,0:T(8,128)(2,1)S(1)} %reshape.61.refs_0_), channel_id=1, source_target_pairs={{0,128},{64,192},{128,0},{192,64},{1,129},{65,193},{129,1},{193,65... | collective-permute-start | bytes 921608 | tf_op jit(solution)/shard_map/ppermute | solution.py:25
  87.7 2.0 %collective-permute-start.6 = (bf16[3,80,640]{2,1,0:T(8,128)(2,1)S(1)}, bf16[3,80,640]{2,1,0:T(8,128)(2,1)}, u32[]{:S(2)}, u32[]{:S(2)}) collective-permute-start(bf16[3,80,640]{2,1,0:T(8,128)(2,1)S(1)} %reshape.61.refs_0_), channel_id=1, source_target_pairs={{0,192},{64,0},{128,64},{192,128},{1,193},{65,1},{129,65},{193,129... | collective-permute-start | bytes 921608 | tf_op jit(solution)/shard_map/ppermute | solution.py:25
  89.7 6.3 %collective-permute-done.8.refs_3_ = bf16[3,80,640]{2,1,0:T(8,128)(2,1)S(1)} collective-permute-done((bf16[3,80,640]{2,1,0:T(8,128)(2,1)S(1)}, bf16[3,80,640]{2,1,0:T(8,128)(2,1)S(1)}, u32[]{:S(2)}, u32[]{:S(2)}) %collective-permute-start.8) | collective-permute-done | bytes 307232 | tf_op jit(solution)/shard_map/ppermute | solution.py:25
  96.1 3.1 %collective-permute-done.7.refs_2_ = bf16[3,80,640]{2,1,0:T(8,128)(2,1)} collective-permute-done((bf16[3,80,640]{2,1,0:T(8,128)(2,1)S(1)}, bf16[3,80,640]{2,1,0:T(8,128)(2,1)}, u32[]{:S(2)}, u32[]{:S(2)}) %collective-permute-start.7) | collective-permute-done | bytes 307232 | tf_op jit(solution)/shard_map/ppermute | solution.py:25
  99.3 8.9 %apply.1 = (f32[2048,640]{1,0:T(8,128)}, f32[16,128]{1,0:T(8,128)S(1)}, f32[3,640]{1,0:T(4,128)S(1)}) custom-call(bf16[2048,640]{1,0:T(8,128)(2,1)S(1)} %copy-done.2, f32[3,640]{1,0:T(4,128)S(1)} %add_add_fusion.osq_ref, bf16[3,80,640]{2,1,0:T(8,128)(2,1)S(1)} %reshape.61.refs_0_, bf16[3,80,640]{2,1,0:T(8,128)(2,1)} %collective-permute-done.6.refs_1_, ...), custom_call_target="tpu_custom_call" | custom-call | flops 3019898880 | bytes 7864320 | tf_op jit(solution)/shard_map/apply/pallas_call | solution.py:176
  108.2 1.2 collective-permute-done.9
  109.3 1.6 %collective-permute-start.12 = (f32[2048]{0:T(1024)S(1)}, f32[2048]{0:T(1024)S(1)}, u32[]{:S(2)}, u32[]{:S(2)}) collective-permute-start(f32[2048]{0:T(1024)S(1)} %bitcast_add_fusion), channel_id=1, source_target_pairs={{0,2},{2,4},{4,6},{6,0},{1,3},{3,5},{5,7},{7,1},{8,10},{10,12},{12... | collective-permute-start | bytes 24584 | tf_op jit(solution)/shard_map/ppermute | solution.py:25
  110.9 1.7 %collective-permute-start.11 = (f32[2048]{0:T(1024)S(1)}, f32[2048]{0:T(1024)S(1)}, u32[]{:S(2)}, u32[]{:S(2)}) collective-permute-start(f32[2048]{0:T(1024)S(1)} %bitcast_add_fusion), channel_id=1, source_target_pairs={{0,6},{2,0},{4,2},{6,4},{1,7},{3,1},{5,3},{7,5},{8,14},{10,8},{12,... | collective-permute-start | bytes 24584 | tf_op jit(solution)/shard_map/ppermute | solution.py:25
  112.6 2.0 %collective-permute-start.10 = (f32[2048]{0:T(1024)S(1)}, f32[2048]{0:T(1024)S(1)}, u32[]{:S(2)}, u32[]{:S(2)}) collective-permute-start(f32[2048]{0:T(1024)S(1)} %bitcast_add_fusion), channel_id=1, source_target_pairs={{0,4},{2,6},{4,0},{6,2},{1,5},{3,7},{5,1},{7,3},{8,12},{10,14},{12... | collective-permute-start | bytes 24584 | tf_op jit(solution)/shard_map/ppermute | solution.py:25
  117.7 4.0 %scale.1 = bf16[2048,640]{1,0:T(8,128)(2,1)} custom-call(f32[2048,640]{1,0:T(8,128)} %get-tuple-element.29.o_ref, f32[1,640]{1,0:T(1,128)S(1)} %reshape.62.gain_ref, f32[16,128]{1,0:T(8,128)S(1)} %bitcast.15, f32[16,128]{1,0:T(8,128)S(1)} %bitcast.18, f32[16,128]{1,0:T(8,128)S(1)} %bitcast.17, f32[16,128]{1,0:T(8,128)S(1)} %bitcast.16), custom_call_target="tpu_custom_call" | custom-call | tf_op jit(solution)/shard_map/scale/pallas_call | solution.py:216
  (46 shorter events, 4.6 us)
Async XLA Ops:
  0.6 28.0 %copy-start = (bf16[2048,640]{1,0:T(8,128)(2,1)S(1)}, bf16[2048,640]{1,0:T(8,128)(2,1)}, u32[]{:S(2)}) copy-start(bf16[2048,640]{1,0:T(8,128)(2,1)} %k_ref.5) | copy-start | bytes 7864324
  0.6 28.0 %copy-start.3 = (f32[2048,2]{0,1:T(2,128)S(1)}, f32[2048,2]{0,1:T(2,128)}, u32[]{:S(2)}) copy-start(f32[2048,2]{0,1:T(2,128)} %param.11) | copy-start | bytes 49156
  24.4 11.8 %collective-permute-start = (bf16[3,80,640]{2,1,0:T(8,128)(2,1)S(1)}, bf16[3,80,640]{2,1,0:T(8,128)(2,1)S(1)}, u32[]{:S(2)}, u32[]{:S(2)}) collective-permute-start(bf16[3,80,640]{2,1,0:T(8,128)(2,1)S(1)} %reshape.57.refs_0_), channel_id=1, source_target_pairs={{0,128},{64,192},{128,0},{192,64},{1,129},{65,193},{129,1},{193,65... | collective-permute-start | bytes 921608 | tf_op jit(solution)/shard_map/ppermute | solution.py:25
  26.6 15.5 %collective-permute-start.2 = (bf16[3,80,640]{2,1,0:T(8,128)(2,1)S(1)}, bf16[3,80,640]{2,1,0:T(8,128)(2,1)S(1)}, u32[]{:S(2)}, u32[]{:S(2)}) collective-permute-start(bf16[3,80,640]{2,1,0:T(8,128)(2,1)S(1)} %reshape.57.refs_0_), channel_id=1, source_target_pairs={{0,64},{64,128},{128,192},{192,0},{1,65},{65,129},{129,193},{193,1... | collective-permute-start | bytes 921608 | tf_op jit(solution)/shard_map/ppermute | solution.py:25
  26.6 15.5 %collective-permute-start.1 = (bf16[3,80,640]{2,1,0:T(8,128)(2,1)S(1)}, bf16[3,80,640]{2,1,0:T(8,128)(2,1)S(1)}, u32[]{:S(2)}, u32[]{:S(2)}) collective-permute-start(bf16[3,80,640]{2,1,0:T(8,128)(2,1)S(1)} %reshape.57.refs_0_), channel_id=1, source_target_pairs={{0,192},{64,0},{128,64},{192,128},{1,193},{65,1},{129,65},{193,129... | collective-permute-start | bytes 921608 | tf_op jit(solution)/shard_map/ppermute | solution.py:25
  28.7 1.7 %copy-start.1 = (bf16[2048,640]{1,0:T(8,128)(2,1)S(1)}, bf16[2048,640]{1,0:T(8,128)(2,1)}, u32[]{:S(2)}) copy-start(bf16[2048,640]{1,0:T(8,128)(2,1)} %v_ref.5) | copy-start | bytes 7864324
  39.9 9.9 %collective-permute-start.3 = (bf16[3,80,640]{2,1,0:T(8,128)(2,1)S(1)}, bf16[3,80,640]{2,1,0:T(8,128)(2,1)S(1)}, u32[]{:S(2)}, u32[]{:S(2)}) collective-permute-start(bf16[3,80,640]{2,1,0:T(8,128)(2,1)S(1)} %get-tuple-element.23), channel_id=1, source_target_pairs={{0,128},{64,192},{128,0},{192,64},{1,129},{65,193},{129,1},{193,65... | collective-permute-start | bytes 921608 | tf_op jit(solution)/shard_map/ppermute | solution.py:25
  47.7 7.3 %collective-permute-start.4 = (bf16[3,80,640]{2,1,0:T(8,128)(2,1)S(1)}, bf16[3,80,640]{2,1,0:T(8,128)(2,1)S(1)}, u32[]{:S(2)}, u32[]{:S(2)}) collective-permute-start(bf16[3,80,640]{2,1,0:T(8,128)(2,1)S(1)} %get-tuple-element.27), channel_id=1, source_target_pairs={{0,64},{64,128},{128,192},{192,0},{1,65},{65,129},{129,193},{193,1... | collective-permute-start | bytes 921608 | tf_op jit(solution)/shard_map/ppermute | solution.py:25
  47.8 7.3 %collective-permute-start.5 = (bf16[3,80,640]{2,1,0:T(8,128)(2,1)S(1)}, bf16[3,80,640]{2,1,0:T(8,128)(2,1)S(1)}, u32[]{:S(2)}, u32[]{:S(2)}) collective-permute-start(bf16[3,80,640]{2,1,0:T(8,128)(2,1)S(1)} %get-tuple-element.28), channel_id=1, source_target_pairs={{0,192},{64,0},{128,64},{192,128},{1,193},{65,1},{129,65},{193,129... | collective-permute-start | bytes 921608 | tf_op jit(solution)/shard_map/ppermute | solution.py:25
  49.9 21.4 %copy-start.4 = (bf16[30,640]{1,0:T(8,128)(2,1)S(1)}, bf16[30,640]{1,0:T(8,128)(2,1)}, u32[]{:S(2)}) copy-start(bf16[30,640]{1,0:T(8,128)(2,1)} %get-tuple-element.26) | copy-start | bytes 115204
  55.4 34.3 %copy-start.5 = (f32[640]{0:T(1024)S(1)}, f32[640]{0:T(1024)}, u32[]{:S(2)}) copy-start(f32[640]{0:T(1024)} %param.15) | copy-start | bytes 7684
  55.4 43.9 %copy-start.2 = (bf16[2048,640]{1,0:T(8,128)(2,1)S(1)}, bf16[2048,640]{1,0:T(8,128)(2,1)}, u32[]{:S(2)}) copy-start(bf16[2048,640]{1,0:T(8,128)(2,1)} %q_ref.1) | copy-start | bytes 7864324
  85.5 10.5 %collective-permute-start.8 = (bf16[3,80,640]{2,1,0:T(8,128)(2,1)S(1)}, bf16[3,80,640]{2,1,0:T(8,128)(2,1)S(1)}, u32[]{:S(2)}, u32[]{:S(2)}) collective-permute-start(bf16[3,80,640]{2,1,0:T(8,128)(2,1)S(1)} %reshape.61.refs_0_), channel_id=1, source_target_pairs={{0,128},{64,192},{128,0},{192,64},{1,129},{65,193},{129,1},{193,65... | collective-permute-start | bytes 921608 | tf_op jit(solution)/shard_map/ppermute | solution.py:25
  87.7 11.5 %collective-permute-start.7 = (bf16[3,80,640]{2,1,0:T(8,128)(2,1)S(1)}, bf16[3,80,640]{2,1,0:T(8,128)(2,1)}, u32[]{:S(2)}, u32[]{:S(2)}) collective-permute-start(bf16[3,80,640]{2,1,0:T(8,128)(2,1)S(1)} %reshape.61.refs_0_), channel_id=1, source_target_pairs={{0,64},{64,128},{128,192},{192,0},{1,65},{65,129},{129,193},{193,1... | collective-permute-start | bytes 921608 | tf_op jit(solution)/shard_map/ppermute | solution.py:25
  87.7 11.6 %collective-permute-start.6 = (bf16[3,80,640]{2,1,0:T(8,128)(2,1)S(1)}, bf16[3,80,640]{2,1,0:T(8,128)(2,1)}, u32[]{:S(2)}, u32[]{:S(2)}) collective-permute-start(bf16[3,80,640]{2,1,0:T(8,128)(2,1)S(1)} %reshape.61.refs_0_), channel_id=1, source_target_pairs={{0,192},{64,0},{128,64},{192,128},{1,193},{65,1},{129,65},{193,129... | collective-permute-start | bytes 921608 | tf_op jit(solution)/shard_map/ppermute | solution.py:25
  108.2 1.2 collective-permute-start.9
  109.3 7.3 %collective-permute-start.12 = (f32[2048]{0:T(1024)S(1)}, f32[2048]{0:T(1024)S(1)}, u32[]{:S(2)}, u32[]{:S(2)}) collective-permute-start(f32[2048]{0:T(1024)S(1)} %bitcast_add_fusion), channel_id=1, source_target_pairs={{0,2},{2,4},{4,6},{6,0},{1,3},{3,5},{5,7},{7,1},{8,10},{10,12},{12... | collective-permute-start | bytes 24584 | tf_op jit(solution)/shard_map/ppermute | solution.py:25
  110.9 5.8 %collective-permute-start.11 = (f32[2048]{0:T(1024)S(1)}, f32[2048]{0:T(1024)S(1)}, u32[]{:S(2)}, u32[]{:S(2)}) collective-permute-start(f32[2048]{0:T(1024)S(1)} %bitcast_add_fusion), channel_id=1, source_target_pairs={{0,6},{2,0},{4,2},{6,4},{1,7},{3,1},{5,3},{7,5},{8,14},{10,8},{12,... | collective-permute-start | bytes 24584 | tf_op jit(solution)/shard_map/ppermute | solution.py:25
  112.6 5.2 %collective-permute-start.10 = (f32[2048]{0:T(1024)S(1)}, f32[2048]{0:T(1024)S(1)}, u32[]{:S(2)}, u32[]{:S(2)}) collective-permute-start(f32[2048]{0:T(1024)S(1)} %bitcast_add_fusion), channel_id=1, source_target_pairs={{0,4},{2,6},{4,0},{6,2},{1,5},{3,7},{5,1},{7,3},{8,12},{10,14},{12... | collective-permute-start | bytes 24584 | tf_op jit(solution)/shard_map/ppermute | solution.py:25

commit v3 on v2

v3 whole, which is shorter than its diff:
```python
import functools

import jax
import jax.numpy as jnp
from jax import lax
from jax.experimental import pallas as pl
from jax.experimental.pallas import tpu as pltpu
from jax.sharding import Mesh
from jax.sharding import PartitionSpec as P

EPS = 1e-06
X, Z, Y, CORE = 4, 8, 4, 2
DH, FF, HEADS = 320, 320, 16
LOCAL = FF // (X * Z)
BLOCK = FF // X
WIN = 384
LANES = 2 * DH
VMEM = 28 << 20
F32, BF16 = jnp.float32, jnp.bfloat16
NT = (((1,), (1,)), ((), ()))


def shifted(array, axis, by):
    n = lax.axis_size(axis)
    return lax.ppermute(array, axis, [(i, (i - by) % n) for i in range(n)])


def gathered_z(copies):
    every = lax.all_to_all(copies, "z", 0, 0, tiled=True)
    return jnp.moveaxis(every.reshape(Z, 3, LOCAL, LANES), 0, 1).reshape(3, BLOCK, LANES)


def in_turn(value, *first):
    return lax.optimization_barrier((value, *first))[0]


def own_lanes(head):
    lane = lax.broadcasted_iota(jnp.int32, (BLOCK, WIN), 1)
    return lane < DH if head == 0 else lane >= WIN - DH


def side_by_side(first, second):
    lane = lax.broadcasted_iota(jnp.int32, (first.shape[0], WIN - 256), 1)
    middle = jnp.where(lane < DH - 256, first[:, 256:], second[:, : WIN - 256])
    return jnp.concatenate([first[:, :256], middle, second[:, WIN - 256 :]], axis=1)


def update_body(blocks, tile, k_ref, v_ref, r_ref, *refs):
    w_refs, g_refs, (osq_ref, wgu, wd, agu, ad) = refs[:blocks], refs[blocks : 2 * blocks], refs[2 * blocks :]
    units = blocks * BLOCK
    sq = [jnp.zeros((1, LANES), F32) for _ in range(3)]
    for b, w_ref in enumerate(w_refs):
        for m in range(3):
            w = w_ref[m]
            wf = w.astype(F32)
            sq[m] += jnp.sum(wf * wf, axis=0, keepdims=True)
            for h in range(2):
                part = jnp.where(own_lanes(h), w[:, h * 256 : h * 256 + WIN], jnp.zeros((), BF16))
                if m < 2:
                    wgu[h, pl.ds(m * units + b * BLOCK, BLOCK), :] = part
                else:
                    wd[h, pl.ds(b * BLOCK, BLOCK), :] = part
    for m in range(3):
        osq_ref[m : m + 1, :] = sq[m]

    for at in range(0, k_ref.shape[0], tile):
        for h in range(2):
            k = k_ref[at : at + tile, h * 256 : h * 256 + WIN]
            v = v_ref[at : at + tile, h * 256 : h * 256 + WIN]
            rate = r_ref[h : h + 1, at : at + tile]
            gu = lax.dot_general(wgu[h], k, NT, preferred_element_type=F32)
            back = lax.dot_general(wd[h], v, NT, preferred_element_type=F32) * rate
            g, u = gu[:units], gu[units:]
            s = 0.5 * jnp.tanh(0.5 * g) + 0.5
            act = g * s
            slope = s + act * (1.0 - s)
            dgate = (back * u * slope).astype(BF16)
            dup = (back * act).astype(BF16)
            hidden = (act * u * rate).astype(BF16)
            ggu = jnp.dot(jnp.concatenate([dgate, dup], axis=0), k, preferred_element_type=F32)
            gd = jnp.dot(hidden, v, preferred_element_type=F32)
            agu[h] = ggu if at == 0 else agu[h] + ggu
            ad[h] = gd if at == 0 else ad[h] + gd

    for b, g_ref in enumerate(g_refs):
        for m in range(3):
            acc, at = (agu, m * units + b * BLOCK) if m < 2 else (ad, b * BLOCK)
            rows = pl.ds(at, BLOCK)
            g_ref[m] = side_by_side(acc[0, rows, :], acc[1, rows, :]).astype(BF16)


def update(keys, values, rates, blocks, tile=1024):
    tokens, n = keys.shape[0], len(blocks)
    vmem = pl.BlockSpec(memory_space=pltpu.VMEM)
    outs = pl.pallas_call(
        functools.partial(update_body, n, tile),
        in_specs=[vmem] * (3 + n),
        out_specs=[vmem] * (n + 1),
        out_shape=[jax.ShapeDtypeStruct((3, BLOCK, LANES), BF16)] * n + [jax.ShapeDtypeStruct((3, LANES), F32)],
        scratch_shapes=[
            pltpu.VMEM((2, 2 * n * BLOCK, WIN), BF16),
            pltpu.VMEM((2, n * BLOCK, WIN), BF16),
            pltpu.VMEM((2, 2 * n * BLOCK, WIN), F32),
            pltpu.VMEM((2, n * BLOCK, WIN), F32),
        ],
        cost_estimate=pl.CostEstimate(
            flops=48 * tokens * n * BLOCK * WIN, bytes_accessed=4 * tokens * LANES, transcendentals=2 * tokens * FF
        ),
        compiler_params=pltpu.CompilerParams(vmem_limit_bytes=VMEM),
        name="update",
    )(keys, values, rates, *blocks)
    return outs[:n], outs[n]


def apply_body(part, q_in, osq_ref, *refs):
    u_in, (o_ref, sq_ref, sc_ref, wgu, wd, q_ref, u_refs, q_sems, u_sems) = refs[:X], refs[X:]
    tokens = q_in.shape[0]
    fetches = [pltpu.make_async_copy(u, u_refs.at[b], u_sems.at[b]) for b, u in enumerate(u_in)]
    reads = [
        pltpu.make_async_copy(q_in.at[r : r + part, :], q_ref.at[r : r + part, :], q_sems.at[r // part])
        for r in range(0, tokens, part)
    ]
    for copy in fetches + reads:
        copy.start()
    wgu[:, FF:WIN, :] = jnp.zeros((2, WIN - FF, WIN), BF16)
    wgu[:, WIN + FF :, :] = jnp.zeros((2, WIN - FF, WIN), BF16)
    wd[:, FF:, :] = jnp.zeros((2, WIN - FF, WIN), BF16)
    for fetch in fetches:
        fetch.wait()
    for m in range(3):
        sq = jnp.zeros((1, LANES), F32)
        for b in range(X):
            wf = u_refs[b, m].astype(F32)
            sq += jnp.sum(wf * wf, axis=0, keepdims=True)
        sc = jnp.sqrt(osq_ref[m : m + 1, :]) * lax.rsqrt(sq + EPS)
        sc_ref[m : m + 1, :] = sc
        for b in range(X):
            for h in range(2):
                cols = slice(h * 256, h * 256 + WIN)
                if m < 2:
                    scaled = (u_refs[b, m, :, cols].astype(F32) * sc[:, cols]).astype(BF16)
                    scaled = jnp.where(own_lanes(h), scaled, jnp.zeros((), BF16))
                    wgu[h, pl.ds(m * WIN + b * BLOCK, BLOCK), :] = scaled
                else:
                    wd[h, pl.ds(b * BLOCK, BLOCK), :] = u_refs[b, m, :, cols]
    down = sc_ref[2:3, :]

    def project(rows, h):
        if h == 0:
            reads[rows.start // part].wait()
        q = q_ref[rows, h * 256 : h * 256 + WIN]
        return lax.dot_general(q, wgu[h], NT, preferred_element_type=F32)

    def finish(rows, outs):
        o = side_by_side(*outs) * down
        o_ref[rows, :] = o.astype(BF16)
        sq = o * o
        sq = sum(sq[:, c * 128 : (c + 1) * 128] for c in range(1, LANES // 128)) + sq[:, :128]
        for j in range(o.shape[0] // 128):
            at = rows.start // 128 + j
            sq_ref[at : at + 1, :] = jnp.sum(jnp.transpose(sq[j * 128 : (j + 1) * 128]), axis=0, keepdims=True)

    steps = [(slice(r, r + part), h) for r in range(0, tokens, part) for h in range(2)]
    ahead, outs = project(*steps[0]), []
    for i, (rows, h) in enumerate(steps):
        g, u = ahead[:, :WIN], ahead[:, WIN:]
        if i + 1 < len(steps):
            ahead = project(*steps[i + 1])
        mixed = (g * (0.5 * jnp.tanh(0.5 * g) + 0.5) * u).astype(BF16)
        outs.append(jnp.dot(mixed, wd[h], preferred_element_type=F32))
        if h == 1:
            finish(rows, outs)
            outs = []


def apply(queries, old_sq, blocks, part=512):
    tokens = queries.shape[0]
    vmem, hbm = pl.BlockSpec(memory_space=pltpu.VMEM), pl.BlockSpec(memory_space=pltpu.HBM)
    return pl.pallas_call(
        functools.partial(apply_body, part),
        in_specs=[hbm, vmem] + [hbm] * X,
        out_specs=[vmem] * 3,
        out_shape=[
            jax.ShapeDtypeStruct((tokens, LANES), BF16),
            jax.ShapeDtypeStruct((tokens // 128, 128), F32),
            jax.ShapeDtypeStruct((3, LANES), F32),
        ],
        scratch_shapes=[
            pltpu.VMEM((2, 2 * WIN, WIN), BF16),
            pltpu.VMEM((2, WIN, WIN), BF16),
            pltpu.VMEM((tokens, LANES), BF16),
            pltpu.VMEM((X, 3, BLOCK, LANES), BF16),
            pltpu.SemaphoreType.DMA((tokens // part,)),
            pltpu.SemaphoreType.DMA((X,)),
        ],
        cost_estimate=pl.CostEstimate(
            flops=12 * tokens * FF * WIN, bytes_accessed=6 * tokens * LANES, transcendentals=2 * tokens * FF
        ),
        compiler_params=pltpu.CompilerParams(vmem_limit_bytes=VMEM),
        name="apply",
    )(queries, old_sq, *blocks)


def scale_body(part, o_ref, gain_ref, *refs):
    sq_refs, (out_ref, out_vmem, sems) = refs[:X], refs[X:]
    spans = [slice(r, r + part) for r in range(0, o_ref.shape[0], part)]
    gain = gain_ref[...]
    sq = sum(r[...] for r in sq_refs[1:]) + sq_refs[0][...]
    scale = lax.rsqrt(sq / (HEADS * DH) + EPS)
    writes = []
    for i, span in enumerate(spans):
        for at in range(span.start, span.stop, 128):
            rows = slice(at, at + 128)
            across = jnp.transpose(jnp.broadcast_to(scale[at // 128 : at // 128 + 1], (128, 128)))
            for c in range(LANES // 128):
                cols = slice(c * 128, (c + 1) * 128)
                out_vmem[rows, cols] = (o_ref[rows, cols].astype(F32) * across * gain[:, cols]).astype(BF16)
        write = pltpu.make_async_copy(out_vmem.at[span, :], out_ref.at[span, :], sems.at[i])
        write.start()
        writes.append(write)
    for write in writes:
        write.wait()


def scaled_output(o, squares, gain, part=256):
    tokens = o.shape[0]
    vmem, hbm = pl.BlockSpec(memory_space=pltpu.VMEM), pl.BlockSpec(memory_space=pltpu.HBM)
    return pl.pallas_call(
        functools.partial(scale_body, part),
        in_specs=[vmem] * (2 + len(squares)),
        out_specs=hbm,
        out_shape=jax.ShapeDtypeStruct((tokens, LANES), BF16),
        scratch_shapes=[
            pltpu.VMEM((tokens, LANES), BF16),
            pltpu.SemaphoreType.DMA((tokens // part,)),
        ],
        compiler_params=pltpu.CompilerParams(vmem_limit_bytes=VMEM),
        name="scale",
    )(o, gain, *squares)


def pack_body(gate_ref, up_ref, down_ref, own_ref, copies_ref):
    rows = []
    for w_ref in (gate_ref, up_ref, down_ref):
        w = w_ref[...].astype(F32)
        rows.append(jnp.concatenate([w[:, 0, :], w[:, 1, :]], axis=1))
    own = jnp.concatenate(rows, axis=0).astype(BF16)
    own_ref[...] = own
    for z in range(Z):
        copies_ref[z] = own


def packed(weights):
    return pl.pallas_call(
        pack_body,
        out_shape=[
            jax.ShapeDtypeStruct((3 * LOCAL, LANES), BF16),
            jax.ShapeDtypeStruct((Z, 3 * LOCAL, LANES), BF16),
        ],
        name="pack",
    )(*weights)


def per_device(keys, values, queries, rates, w_gate, w_up, w_down, gain):
    own, copies = packed((w_gate, w_up, w_down))
    rates = rates.T
    here = gathered_z(copies)
    across = shifted(here, "x", 2)
    sides = shifted(here, "x", 1), shifted(here, "x", 3)
    (g0,), sq_a = update(keys, values, rates, (here,))
    (g2,), sq_b = update(keys, values, in_turn(rates, g0), (across,))
    r2 = shifted(g2, "x", 2)
    (g1, g3), sq_c = update(keys, values, in_turn(rates, g2), sides)
    r1, r3 = shifted(g1, "x", 3), shifted(g3, "x", 1)
    total = lax.optimization_barrier(g0.astype(F32) + r2.astype(F32)) + r1.astype(F32) + r3.astype(F32)
    old_sq = sq_a + sq_b + sq_c
    pieces = jnp.moveaxis(total.astype(BF16).reshape(3, Z, LOCAL, LANES), 1, 0).reshape(Z, 3 * LOCAL, LANES)
    pieces = lax.all_to_all(pieces, "z", 0, 0, tiled=True)
    updated = own.astype(F32) + jnp.sum(pieces.astype(F32), axis=0)

    here = gathered_z(jnp.broadcast_to(updated.astype(BF16)[None], (Z, 3 * LOCAL, LANES)))
    new = [here] + [shifted(here, "x", s) for s in (1, 3, 2)]
    queries, *new[1:3] = (pltpu.with_memory_space_constraint(a, pltpu.HBM) for a in (queries, *new[1:3]))
    o, squares, scale = apply(queries, old_sq, new)
    squares = squares.reshape(-1)
    squares += shifted(squares, "core", 1)
    squares = [squares] + [shifted(squares, "y", s) for s in (2, 1, 3)]
    output = scaled_output(o, [s.reshape(-1, 128) for s in squares], gain.reshape(1, LANES))
    fresh = (updated.reshape(3, LOCAL, LANES) * scale[:, None, :]).astype(BF16).reshape(3, LOCAL, 2, DH)
    return output, fresh[0], fresh[1], fresh[2]


def solution(mesh):
    split = Mesh(mesh.devices.reshape(X, Z, Y, CORE), ("x", "z", "y", "core"))
    ctx, head = ("x", "z"), ("y", "core")
    weight = P(ctx, head, None)
    return jax.shard_map(
        per_device,
        mesh=split,
        in_specs=(P(ctx, head),) * 4 + (weight,) * 3 + (P(head),),
        out_specs=(P(ctx, head),) + (weight,) * 3,
        check_vma=False,
    )
```

time: 122 us -> 119 us (0.975)
  Pallas kernels: 27.5 us -> 23.3 us
    pallas_call x5, Pallas kernels: 25.8 us -> 21.6 us  [the longest x3 11.8 us: update(): pl.pallas_call(functools.partial(update_body, n, tile), in_specs=[vmem] *...]
  transfers between devices with their start and end apart: 13 -> 13, of which waited for: 8 -> 7; matrix products, arithmetic and copies ran while one was open for 2% -> 2% of each run, Pallas kernels for 11% -> 10%
where the time goes in v3:
time: 119 us
  blocking collectives  51.3 us (43%)
  Pallas kernels  23.3 us (20%)
  waiting for transfers between devices  20.2 us (17%)
  starting transfers between devices  17.3 us (15%)
  local copies, waits for them, and re-layouts  5.36 us (5%)
    all_to_all x2, blocking collectives, gathered_z(): every = lax.all_to_all(copies, 'z', 0, 0, tiled=True)  36 us
    ppermute x13, waiting for transfers between devices, shifted(): return lax.ppermute(array, axis, [(i, (i - by) % n) for i in range(n)])  20.2 us
    ppermute x13, starting transfers between devices, shifted(): return lax.ppermute(array, axis, [(i, (i - by) % n) for i in range(n)])  17.3 us
    all_to_all x1, blocking collectives, per_device(): pieces = lax.all_to_all(pieces, 'z', 0, 0, tiled=True)  15.3 us
    pallas_call x3, Pallas kernels, update(): pl.pallas_call(functools.partial(update_body, n, tile), in_specs=[vmem] *...  11.8 us
    pallas_call x1, Pallas kernels, apply(): pl.pallas_call(functools.partial(apply_body, part), in_specs=[hbm, vmem]...  8.02 us
    unnamed x12, local copies, waits for them, and re-layouts  2.48 us
  transfers between devices with their start and end apart: 13, of which 7 were waited for; matrix products, arithmetic and copies ran while one was open for 2% of the time, Pallas kernels for 10%

profile of v3, /device:TPU:2, one launch (start us, length us, event | category | flops | bytes accessed | tf_op | source)
XLA Modules:
  0.0 118.8 jit_solution(5588942244913073632)
XLA Ops:
  0.7 1.7 %pack.1 = (bf16[30,640]{1,0:T(8,128)(2,1)}, bf16[8,30,640]{2,1,0:T(8,128)(2,1)}) custom-call(bf16[10,2,320]{2,1,0:T(2,128)(2,1)} %gate_ref.1, bf16[10,2,320]{2,1,0:T(2,128)(2,1)} %up_ref.1, bf16[10,2,320]{2,1,0:T(2,128)(2,1)} %down_ref.1), custom_call_target="tpu_custom_call" | custom-call | tf_op jit(solution)/shard_map/pack/pallas_call | solution.py:254
  2.4 21.7 %all_to_all.15 = bf16[8,30,640]{2,1,0:T(8,128)(2,1)S(1)} all-to-all(bf16[8,30,640]{2,1,0:T(8,128)(2,1)} %get-tuple-element.18), channel_id=1, replica_groups=mesh['x'=4,'z'=8,'y'=4,'core'=2] {'z'}, dimensions={0} | all-to-all | bytes 614400 | tf_op jit(solution)/shard_map/all_to_all | solution.py:29
  24.4 2.2 %collective-permute-start = (bf16[3,80,640]{2,1,0:T(8,128)(2,1)S(1)}, bf16[3,80,640]{2,1,0:T(8,128)(2,1)S(1)}, u32[]{:S(2)}, u32[]{:S(2)}) collective-permute-start(bf16[3,80,640]{2,1,0:T(8,128)(2,1)S(1)} %reshape.57.refs_0_), channel_id=1, source_target_pairs={{0,128},{64,192},{128,0},{192,64},{1,129},{65,193},{129,1},{193,65... | collective-permute-start | bytes 921608 | tf_op jit(solution)/shard_map/ppermute | solution.py:25
  26.6 2.0 %collective-permute-start.1 = (bf16[3,80,640]{2,1,0:T(8,128)(2,1)S(1)}, bf16[3,80,640]{2,1,0:T(8,128)(2,1)S(1)}, u32[]{:S(2)}, u32[]{:S(2)}) collective-permute-start(bf16[3,80,640]{2,1,0:T(8,128)(2,1)S(1)} %reshape.57.refs_0_), channel_id=1, source_target_pairs={{0,192},{64,0},{128,64},{192,128},{1,193},{65,1},{129,65},{193,129... | collective-permute-start | bytes 921608 | tf_op jit(solution)/shard_map/ppermute | solution.py:25
  28.7 1.7 %copy-done.1 = bf16[2048,640]{1,0:T(8,128)(2,1)S(1)} copy-done((bf16[2048,640]{1,0:T(8,128)(2,1)S(1)}, bf16[2048,640]{1,0:T(8,128)(2,1)}, u32[]{:S(2)}) %copy-start.1) | copy-done | bytes 2621464
  30.4 3.4 %update.3 = (bf16[3,80,640]{2,1,0:T(8,128)(2,1)S(1)}, f32[3,640]{1,0:T(4,128)S(1)}) custom-call(bf16[2048,640]{1,0:T(8,128)(2,1)S(1)} %copy-done, bf16[2048,640]{1,0:T(8,128)(2,1)S(1)} %copy-done.1, f32[2,2048]{1,0:T(2,128)S(1)} %bitcast.20, bf16[3,80,640]{2,1,0:T(8,128)(2,1)S(1)} %reshape.57.refs_0_), custom_call_target="tpu_custom_call" | custom-call | flops 3019898880 | bytes 5242880 | tf_op jit(solution)/shard_map/update/pallas_call | solution.py:95
  33.8 2.5 %collective-permute-done.refs_0_ = bf16[3,80,640]{2,1,0:T(8,128)(2,1)S(1)} collective-permute-done((bf16[3,80,640]{2,1,0:T(8,128)(2,1)S(1)}, bf16[3,80,640]{2,1,0:T(8,128)(2,1)S(1)}, u32[]{:S(2)}, u32[]{:S(2)}) %collective-permute-start) | collective-permute-done | bytes 307232 | tf_op jit(solution)/shard_map/ppermute | solution.py:25
  36.2 3.4 %update.4 = (bf16[3,80,640]{2,1,0:T(8,128)(2,1)S(1)}, f32[3,640]{1,0:T(4,128)S(1)}) custom-call(bf16[2048,640]{1,0:T(8,128)(2,1)S(1)} %copy-done, bf16[2048,640]{1,0:T(8,128)(2,1)S(1)} %copy-done.1, f32[2,2048]{1,0:T(2,128)S(1)} %bitcast.21, bf16[3,80,640]{2,1,0:T(8,128)(2,1)S(1)} %collective-permute-done.refs_0_), custom_call_target="tpu_custom_call" | custom-call | flops 3019898880 | bytes 5242880 | tf_op jit(solution)/shard_map/update/pallas_call | solution.py:95
  39.6 2.4 %collective-permute-start.3 = (bf16[3,80,640]{2,1,0:T(8,128)(2,1)S(1)}, bf16[3,80,640]{2,1,0:T(8,128)(2,1)S(1)}, u32[]{:S(2)}, u32[]{:S(2)}) collective-permute-start(bf16[3,80,640]{2,1,0:T(8,128)(2,1)S(1)} %get-tuple-element.23), channel_id=1, source_target_pairs={{0,128},{64,192},{128,0},{192,64},{1,129},{65,193},{129,1},{193,65... | collective-permute-start | bytes 921608 | tf_op jit(solution)/shard_map/ppermute | solution.py:25
  42.0 5.1 %update.5 = (bf16[3,80,640]{2,1,0:T(8,128)(2,1)S(1)}, bf16[3,80,640]{2,1,0:T(8,128)(2,1)S(1)}, f32[3,640]{1,0:T(4,128)S(1)}) custom-call(bf16[2048,640]{1,0:T(8,128)(2,1)S(1)} %copy-done, bf16[2048,640]{1,0:T(8,128)(2,1)S(1)} %copy-done.1, f32[2,2048]{1,0:T(2,128)S(1)} %bitcast.22, bf16[3,80,640]{2,1,0:T(8,128)(2,1)S(1)} %collective-permute-done.1.refs_0_, ...), custom_call_target="tpu_custom_call" | custom-call | flops 6039797760 | bytes 5242880 | tf_op jit(solution)/shard_map/update/pallas_call | solution.py:95
  47.2 2.0 %collective-permute-start.5 = (bf16[3,80,640]{2,1,0:T(8,128)(2,1)S(1)}, bf16[3,80,640]{2,1,0:T(8,128)(2,1)S(1)}, u32[]{:S(2)}, u32[]{:S(2)}) collective-permute-start(bf16[3,80,640]{2,1,0:T(8,128)(2,1)S(1)} %get-tuple-element.28), channel_id=1, source_target_pairs={{0,192},{64,0},{128,64},{192,128},{1,193},{65,1},{129,65},{193,129... | collective-permute-start | bytes 921608 | tf_op jit(solution)/shard_map/ppermute | solution.py:25
  49.3 5.7 %collective-permute-done.4 = bf16[3,80,640]{2,1,0:T(8,128)(2,1)S(1)} collective-permute-done((bf16[3,80,640]{2,1,0:T(8,128)(2,1)S(1)}, bf16[3,80,640]{2,1,0:T(8,128)(2,1)S(1)}, u32[]{:S(2)}, u32[]{:S(2)}) %collective-permute-start.4) | collective-permute-done | bytes 307232 | tf_op jit(solution)/shard_map/ppermute | solution.py:25
  55.5 15.3 %all_to_all.16 = bf16[8,30,640]{2,1,0:T(8,128)(2,1)S(1)} all-to-all(bf16[8,30,640]{2,1,0:T(8,128)(2,1)S(1)} %copy.20), channel_id=1, replica_groups=mesh['x'=4,'z'=8,'y'=4,'core'=2] {'z'}, dimensions={0} | all-to-all | bytes 614400 | tf_op jit(solution)/shard_map/all_to_all | solution.py:278
  70.9 14.3 %all_to_all.17 = bf16[8,30,640]{2,1,0:T(8,128)(2,1)S(1)} all-to-all(bf16[8,30,640]{2,1,0:T(8,128)(2,1)S(1)} %broadcast_in_dim.2), channel_id=1, replica_groups=mesh['x'=4,'z'=8,'y'=4,'core'=2] {'z'}, dimensions={0} | all-to-all | bytes 614400 | tf_op jit(solution)/shard_map/all_to_all | solution.py:29
  85.5 1.3 %collective-permute-start.8 = (bf16[3,80,640]{2,1,0:T(8,128)(2,1)S(1)}, bf16[3,80,640]{2,1,0:T(8,128)(2,1)S(1)}, u32[]{:S(2)}, u32[]{:S(2)}) collective-permute-start(bf16[3,80,640]{2,1,0:T(8,128)(2,1)S(1)} %reshape.61.refs_0_), channel_id=1, source_target_pairs={{0,128},{64,192},{128,0},{192,64},{1,129},{65,193},{129,1},{193,65... | collective-permute-start | bytes 921608 | tf_op jit(solution)/shard_map/ppermute | solution.py:25
  86.7 2.0 %collective-permute-start.6 = (bf16[3,80,640]{2,1,0:T(8,128)(2,1)S(1)}, bf16[3,80,640]{2,1,0:T(8,128)(2,1)}, u32[]{:S(2)}, u32[]{:S(2)}) collective-permute-start(bf16[3,80,640]{2,1,0:T(8,128)(2,1)S(1)} %reshape.61.refs_0_), channel_id=1, source_target_pairs={{0,192},{64,0},{128,64},{192,128},{1,193},{65,1},{129,65},{193,129... | collective-permute-start | bytes 921608 | tf_op jit(solution)/shard_map/ppermute | solution.py:25
  88.8 7.0 %collective-permute-done.8.refs_3_ = bf16[3,80,640]{2,1,0:T(8,128)(2,1)S(1)} collective-permute-done((bf16[3,80,640]{2,1,0:T(8,128)(2,1)S(1)}, bf16[3,80,640]{2,1,0:T(8,128)(2,1)S(1)}, u32[]{:S(2)}, u32[]{:S(2)}) %collective-permute-start.8) | collective-permute-done | bytes 307232 | tf_op jit(solution)/shard_map/ppermute | solution.py:25
  95.8 2.7 %collective-permute-done.7.refs_2_ = bf16[3,80,640]{2,1,0:T(8,128)(2,1)S(1)} collective-permute-done((bf16[3,80,640]{2,1,0:T(8,128)(2,1)S(1)}, bf16[3,80,640]{2,1,0:T(8,128)(2,1)S(1)}, u32[]{:S(2)}, u32[]{:S(2)}) %collective-permute-start.7) | collective-permute-done | bytes 307232 | tf_op jit(solution)/shard_map/ppermute | solution.py:25
  99.2 8.0 %apply.1 = (bf16[2048,640]{1,0:T(8,128)(2,1)S(1)}, f32[16,128]{1,0:T(8,128)S(1)}, f32[3,640]{1,0:T(4,128)S(1)}) custom-call(bf16[2048,640]{1,0:T(8,128)(2,1)} %q_in.1, f32[3,640]{1,0:T(4,128)S(1)} %add_add_fusion.osq_ref, bf16[3,80,640]{2,1,0:T(8,128)(2,1)S(1)} %reshape.61.refs_0_, bf16[3,80,640]{2,1,0:T(8,128)(2,1)} %collective-permute-done.6.refs_1_, ...), custom_call_target="tpu_custom_call" | custom-call | flops 3019898880 | bytes 7864320 | tf_op jit(solution)/shard_map/apply/pallas_call | solution.py:179
  107.4 1.1 collective-permute-done.9
  108.5 1.6 %collective-permute-start.12 = (f32[2048]{0:T(1024)S(1)}, f32[2048]{0:T(1024)S(1)}, u32[]{:S(2)}, u32[]{:S(2)}) collective-permute-start(f32[2048]{0:T(1024)S(1)} %bitcast_add_fusion), channel_id=1, source_target_pairs={{0,2},{2,4},{4,6},{6,0},{1,3},{3,5},{5,7},{7,1},{8,10},{10,12},{12... | collective-permute-start | bytes 24584 | tf_op jit(solution)/shard_map/ppermute | solution.py:25
  110.1 1.6 %collective-permute-start.11 = (f32[2048]{0:T(1024)S(1)}, f32[2048]{0:T(1024)S(1)}, u32[]{:S(2)}, u32[]{:S(2)}) collective-permute-start(f32[2048]{0:T(1024)S(1)} %bitcast_add_fusion), channel_id=1, source_target_pairs={{0,6},{2,0},{4,2},{6,4},{1,7},{3,1},{5,3},{7,5},{8,14},{10,8},{12,... | collective-permute-start | bytes 24584 | tf_op jit(solution)/shard_map/ppermute | solution.py:25
  111.8 2.0 %collective-permute-start.10 = (f32[2048]{0:T(1024)S(1)}, f32[2048]{0:T(1024)S(1)}, u32[]{:S(2)}, u32[]{:S(2)}) collective-permute-start(f32[2048]{0:T(1024)S(1)} %bitcast_add_fusion), channel_id=1, source_target_pairs={{0,4},{2,6},{4,0},{6,2},{1,5},{3,7},{5,1},{7,3},{8,12},{10,14},{12... | collective-permute-start | bytes 24584 | tf_op jit(solution)/shard_map/ppermute | solution.py:25
  116.9 1.7 %scale.1 = bf16[2048,640]{1,0:T(8,128)(2,1)} custom-call(bf16[2048,640]{1,0:T(8,128)(2,1)S(1)} %get-tuple-element.29.o_ref, f32[1,640]{1,0:T(1,128)S(1)} %reshape.62.gain_ref, f32[16,128]{1,0:T(8,128)S(1)} %bitcast.15, f32[16,128]{1,0:T(8,128)S(1)} %bitcast.18, f32[16,128]{1,0:T(8,128)S(1)} %bitcast.17, f32[16,128]{1,0:T(8,128)S(1)} %bitcast.16), custom_call_target="tpu_custom_call" | custom-call | tf_op jit(solution)/shard_map/scale/pallas_call | solution.py:228
  (46 shorter events, 5.2 us)
Async XLA Ops:
  0.6 28.0 %copy-start = (bf16[2048,640]{1,0:T(8,128)(2,1)S(1)}, bf16[2048,640]{1,0:T(8,128)(2,1)}, u32[]{:S(2)}) copy-start(bf16[2048,640]{1,0:T(8,128)(2,1)} %k_ref.5) | copy-start | bytes 7864324
  0.6 28.0 %copy-start.2 = (f32[2048,2]{0,1:T(2,128)S(1)}, f32[2048,2]{0,1:T(2,128)}, u32[]{:S(2)}) copy-start(f32[2048,2]{0,1:T(2,128)} %param.11) | copy-start | bytes 49156
  24.4 11.8 %collective-permute-start = (bf16[3,80,640]{2,1,0:T(8,128)(2,1)S(1)}, bf16[3,80,640]{2,1,0:T(8,128)(2,1)S(1)}, u32[]{:S(2)}, u32[]{:S(2)}) collective-permute-start(bf16[3,80,640]{2,1,0:T(8,128)(2,1)S(1)} %reshape.57.refs_0_), channel_id=1, source_target_pairs={{0,128},{64,192},{128,0},{192,64},{1,129},{65,193},{129,1},{193,65... | collective-permute-start | bytes 921608 | tf_op jit(solution)/shard_map/ppermute | solution.py:25
  26.6 15.4 %collective-permute-start.2 = (bf16[3,80,640]{2,1,0:T(8,128)(2,1)S(1)}, bf16[3,80,640]{2,1,0:T(8,128)(2,1)S(1)}, u32[]{:S(2)}, u32[]{:S(2)}) collective-permute-start(bf16[3,80,640]{2,1,0:T(8,128)(2,1)S(1)} %reshape.57.refs_0_), channel_id=1, source_target_pairs={{0,64},{64,128},{128,192},{192,0},{1,65},{65,129},{129,193},{193,1... | collective-permute-start | bytes 921608 | tf_op jit(solution)/shard_map/ppermute | solution.py:25
  26.6 15.4 %collective-permute-start.1 = (bf16[3,80,640]{2,1,0:T(8,128)(2,1)S(1)}, bf16[3,80,640]{2,1,0:T(8,128)(2,1)S(1)}, u32[]{:S(2)}, u32[]{:S(2)}) collective-permute-start(bf16[3,80,640]{2,1,0:T(8,128)(2,1)S(1)} %reshape.57.refs_0_), channel_id=1, source_target_pairs={{0,192},{64,0},{128,64},{192,128},{1,193},{65,1},{129,65},{193,129... | collective-permute-start | bytes 921608 | tf_op jit(solution)/shard_map/ppermute | solution.py:25
  28.7 1.7 %copy-start.1 = (bf16[2048,640]{1,0:T(8,128)(2,1)S(1)}, bf16[2048,640]{1,0:T(8,128)(2,1)}, u32[]{:S(2)}) copy-start(bf16[2048,640]{1,0:T(8,128)(2,1)} %v_ref.5) | copy-start | bytes 7864324
  39.6 9.6 %collective-permute-start.3 = (bf16[3,80,640]{2,1,0:T(8,128)(2,1)S(1)}, bf16[3,80,640]{2,1,0:T(8,128)(2,1)S(1)}, u32[]{:S(2)}, u32[]{:S(2)}) collective-permute-start(bf16[3,80,640]{2,1,0:T(8,128)(2,1)S(1)} %get-tuple-element.23), channel_id=1, source_target_pairs={{0,128},{64,192},{128,0},{192,64},{1,129},{65,193},{129,1},{193,65... | collective-permute-start | bytes 921608 | tf_op jit(solution)/shard_map/ppermute | solution.py:25
  47.1 7.9 %collective-permute-start.4 = (bf16[3,80,640]{2,1,0:T(8,128)(2,1)S(1)}, bf16[3,80,640]{2,1,0:T(8,128)(2,1)S(1)}, u32[]{:S(2)}, u32[]{:S(2)}) collective-permute-start(bf16[3,80,640]{2,1,0:T(8,128)(2,1)S(1)} %get-tuple-element.27), channel_id=1, source_target_pairs={{0,64},{64,128},{128,192},{192,0},{1,65},{65,129},{129,193},{193,1... | collective-permute-start | bytes 921608 | tf_op jit(solution)/shard_map/ppermute | solution.py:25
  47.2 7.9 %collective-permute-start.5 = (bf16[3,80,640]{2,1,0:T(8,128)(2,1)S(1)}, bf16[3,80,640]{2,1,0:T(8,128)(2,1)S(1)}, u32[]{:S(2)}, u32[]{:S(2)}) collective-permute-start(bf16[3,80,640]{2,1,0:T(8,128)(2,1)S(1)} %get-tuple-element.28), channel_id=1, source_target_pairs={{0,192},{64,0},{128,64},{192,128},{1,193},{65,1},{129,65},{193,129... | collective-permute-start | bytes 921608 | tf_op jit(solution)/shard_map/ppermute | solution.py:25
  49.3 21.5 %copy-start.3 = (bf16[30,640]{1,0:T(8,128)(2,1)S(1)}, bf16[30,640]{1,0:T(8,128)(2,1)}, u32[]{:S(2)}) copy-start(bf16[30,640]{1,0:T(8,128)(2,1)} %get-tuple-element.26) | copy-start | bytes 115204
  55.4 33.3 %copy-start.4 = (f32[640]{0:T(1024)S(1)}, f32[640]{0:T(1024)}, u32[]{:S(2)}) copy-start(f32[640]{0:T(1024)} %param.15) | copy-start | bytes 7684
  85.5 10.4 %collective-permute-start.8 = (bf16[3,80,640]{2,1,0:T(8,128)(2,1)S(1)}, bf16[3,80,640]{2,1,0:T(8,128)(2,1)S(1)}, u32[]{:S(2)}, u32[]{:S(2)}) collective-permute-start(bf16[3,80,640]{2,1,0:T(8,128)(2,1)S(1)} %reshape.61.refs_0_), channel_id=1, source_target_pairs={{0,128},{64,192},{128,0},{192,64},{1,129},{65,193},{129,1},{193,65... | collective-permute-start | bytes 921608 | tf_op jit(solution)/shard_map/ppermute | solution.py:25
  86.7 11.8 %collective-permute-start.7 = (bf16[3,80,640]{2,1,0:T(8,128)(2,1)S(1)}, bf16[3,80,640]{2,1,0:T(8,128)(2,1)S(1)}, u32[]{:S(2)}, u32[]{:S(2)}) collective-permute-start(bf16[3,80,640]{2,1,0:T(8,128)(2,1)S(1)} %reshape.61.refs_0_), channel_id=1, source_target_pairs={{0,64},{64,128},{128,192},{192,0},{1,65},{65,129},{129,193},{193,1... | collective-permute-start | bytes 921608 | tf_op jit(solution)/shard_map/ppermute | solution.py:25
  86.7 12.5 %collective-permute-start.6 = (bf16[3,80,640]{2,1,0:T(8,128)(2,1)S(1)}, bf16[3,80,640]{2,1,0:T(8,128)(2,1)}, u32[]{:S(2)}, u32[]{:S(2)}) collective-permute-start(bf16[3,80,640]{2,1,0:T(8,128)(2,1)S(1)} %reshape.61.refs_0_), channel_id=1, source_target_pairs={{0,192},{64,0},{128,64},{192,128},{1,193},{65,1},{129,65},{193,129... | collective-permute-start | bytes 921608 | tf_op jit(solution)/shard_map/ppermute | solution.py:25
  98.5 0.7 copy-start.5
  107.3 1.3 %collective-permute-start.9 = (f32[2048]{0:T(1024)S(1)}, f32[2048]{0:T(1024)S(1)}, u32[]{:S(2)}, u32[]{:S(2)}) collective-permute-start(f32[2048]{0:T(1024)S(1)} %bitcast.19), channel_id=1, source_target_pairs={{0,1},{1,0},{2,3},{3,2},{4,5},{5,4},{6,7},{7,6},{8,9},{9,8},{10,11... | collective-permute-start | bytes 24584 | tf_op jit(solution)/shard_map/ppermute | solution.py:25
  108.5 7.3 %collective-permute-start.12 = (f32[2048]{0:T(1024)S(1)}, f32[2048]{0:T(1024)S(1)}, u32[]{:S(2)}, u32[]{:S(2)}) collective-permute-start(f32[2048]{0:T(1024)S(1)} %bitcast_add_fusion), channel_id=1, source_target_pairs={{0,2},{2,4},{4,6},{6,0},{1,3},{3,5},{5,7},{7,1},{8,10},{10,12},{12... | collective-permute-start | bytes 24584 | tf_op jit(solution)/shard_map/ppermute | solution.py:25
  110.1 5.7 %collective-permute-start.11 = (f32[2048]{0:T(1024)S(1)}, f32[2048]{0:T(1024)S(1)}, u32[]{:S(2)}, u32[]{:S(2)}) collective-permute-start(f32[2048]{0:T(1024)S(1)} %bitcast_add_fusion), channel_id=1, source_target_pairs={{0,6},{2,0},{4,2},{6,4},{1,7},{3,1},{5,3},{7,5},{8,14},{10,8},{12,... | collective-permute-start | bytes 24584 | tf_op jit(solution)/shard_map/ppermute | solution.py:25
  111.8 5.2 %collective-permute-start.10 = (f32[2048]{0:T(1024)S(1)}, f32[2048]{0:T(1024)S(1)}, u32[]{:S(2)}, u32[]{:S(2)}) collective-permute-start(f32[2048]{0:T(1024)S(1)} %bitcast_add_fusion), channel_id=1, source_target_pairs={{0,4},{2,6},{4,0},{6,2},{1,5},{3,7},{5,1},{7,3},{8,12},{10,14},{12... | collective-permute-start | bytes 24584 | tf_op jit(solution)/shard_map/ppermute | solution.py:25

commit v4 on v3

--- a/solution.py
+++ b/solution.py
@@ -280,7 +280,9 @@
 
     here = gathered_z(jnp.broadcast_to(updated.astype(BF16)[None], (Z, 3 * LOCAL, LANES)))
     new = [here] + [shifted(here, "x", s) for s in (1, 3, 2)]
-    queries, *new[1:3] = (pltpu.with_memory_space_constraint(a, pltpu.HBM) for a in (queries, *new[1:3]))
+    queries = pltpu.with_memory_space_constraint(queries, pltpu.HBM)
+    new[1] = pltpu.with_memory_space_constraint(new[1], pltpu.HBM)
+    new[3] = pltpu.with_memory_space_constraint(new[3], pltpu.HBM)
     o, squares, scale = apply(queries, old_sq, new)
     squares = squares.reshape(-1)
     squares += shifted(squares, "core", 1)

time: 119 us -> 120 us (level)
  transfers between devices with their start and end apart: 13 -> 13, of which waited for: 7 -> 8; matrix products, arithmetic and copies ran while one was open for 2% -> 2% of each run, Pallas kernels for 10% -> 10%
where the time goes in v4:
time: 120 us; the launch traced here: 119 us
  blocking collectives  51.3 us (43%)
  Pallas kernels  23.9 us (20%)
  waiting for transfers between devices  20.7 us (17%)
  starting transfers between devices  17.3 us (14%)
  local copies, waits for them, and re-layouts  4.64 us (4%)
    all_to_all x2, blocking collectives, gathered_z(): every = lax.all_to_all(copies, 'z', 0, 0, tiled=True)  36 us
    ppermute x13, waiting for transfers between devices, shifted(): return lax.ppermute(array, axis, [(i, (i - by) % n) for i in range(n)])  20.7 us
    ppermute x13, starting transfers between devices, shifted(): return lax.ppermute(array, axis, [(i, (i - by) % n) for i in range(n)])  17.3 us
    all_to_all x1, blocking collectives, per_device(): pieces = lax.all_to_all(pieces, 'z', 0, 0, tiled=True)  15.3 us
    pallas_call x3, Pallas kernels, update(): pl.pallas_call(functools.partial(update_body, n, tile), in_specs=[vmem] *...  11.8 us
    pallas_call x1, Pallas kernels, apply(): pl.pallas_call(functools.partial(apply_body, part), in_specs=[hbm, vmem]...  8.63 us
  transfers between devices with their start and end apart: 13, of which 8 were waited for; matrix products, arithmetic and copies ran while one was open for 2% of the time, Pallas kernels for 10%

profile of v4, /device:TPU:2, one launch (start us, length us, event | category | flops | bytes accessed | tf_op | source)
XLA Modules:
  0.0 119.3 jit_solution(6493627025203623565)
XLA Ops:
  0.7 1.7 %pack.1 = (bf16[30,640]{1,0:T(8,128)(2,1)}, bf16[8,30,640]{2,1,0:T(8,128)(2,1)}) custom-call(bf16[10,2,320]{2,1,0:T(2,128)(2,1)} %gate_ref.1, bf16[10,2,320]{2,1,0:T(2,128)(2,1)} %up_ref.1, bf16[10,2,320]{2,1,0:T(2,128)(2,1)} %down_ref.1), custom_call_target="tpu_custom_call" | custom-call | tf_op jit(solution)/shard_map/pack/pallas_call | solution.py:254
  2.4 21.7 %all_to_all.15 = bf16[8,30,640]{2,1,0:T(8,128)(2,1)S(1)} all-to-all(bf16[8,30,640]{2,1,0:T(8,128)(2,1)} %get-tuple-element.18), channel_id=1, replica_groups=mesh['x'=4,'z'=8,'y'=4,'core'=2] {'z'}, dimensions={0} | all-to-all | bytes 614400 | tf_op jit(solution)/shard_map/all_to_all | solution.py:29
  24.4 2.2 %collective-permute-start = (bf16[3,80,640]{2,1,0:T(8,128)(2,1)S(1)}, bf16[3,80,640]{2,1,0:T(8,128)(2,1)S(1)}, u32[]{:S(2)}, u32[]{:S(2)}) collective-permute-start(bf16[3,80,640]{2,1,0:T(8,128)(2,1)S(1)} %reshape.57.refs_0_), channel_id=1, source_target_pairs={{0,128},{64,192},{128,0},{192,64},{1,129},{65,193},{129,1},{193,65... | collective-permute-start | bytes 921608 | tf_op jit(solution)/shard_map/ppermute | solution.py:25
  26.6 2.0 %collective-permute-start.1 = (bf16[3,80,640]{2,1,0:T(8,128)(2,1)S(1)}, bf16[3,80,640]{2,1,0:T(8,128)(2,1)S(1)}, u32[]{:S(2)}, u32[]{:S(2)}) collective-permute-start(bf16[3,80,640]{2,1,0:T(8,128)(2,1)S(1)} %reshape.57.refs_0_), channel_id=1, source_target_pairs={{0,192},{64,0},{128,64},{192,128},{1,193},{65,1},{129,65},{193,129... | collective-permute-start | bytes 921608 | tf_op jit(solution)/shard_map/ppermute | solution.py:25
  28.7 1.7 %copy-done.1 = bf16[2048,640]{1,0:T(8,128)(2,1)S(1)} copy-done((bf16[2048,640]{1,0:T(8,128)(2,1)S(1)}, bf16[2048,640]{1,0:T(8,128)(2,1)}, u32[]{:S(2)}) %copy-start.1) | copy-done | bytes 2621464
  30.4 3.4 %update.3 = (bf16[3,80,640]{2,1,0:T(8,128)(2,1)S(1)}, f32[3,640]{1,0:T(4,128)S(1)}) custom-call(bf16[2048,640]{1,0:T(8,128)(2,1)S(1)} %copy-done, bf16[2048,640]{1,0:T(8,128)(2,1)S(1)} %copy-done.1, f32[2,2048]{1,0:T(2,128)S(1)} %bitcast.20, bf16[3,80,640]{2,1,0:T(8,128)(2,1)S(1)} %reshape.57.refs_0_), custom_call_target="tpu_custom_call" | custom-call | flops 3019898880 | bytes 5242880 | tf_op jit(solution)/shard_map/update/pallas_call | solution.py:95
  33.8 2.5 %collective-permute-done.refs_0_ = bf16[3,80,640]{2,1,0:T(8,128)(2,1)S(1)} collective-permute-done((bf16[3,80,640]{2,1,0:T(8,128)(2,1)S(1)}, bf16[3,80,640]{2,1,0:T(8,128)(2,1)S(1)}, u32[]{:S(2)}, u32[]{:S(2)}) %collective-permute-start) | collective-permute-done | bytes 307232 | tf_op jit(solution)/shard_map/ppermute | solution.py:25
  36.2 3.4 %update.4 = (bf16[3,80,640]{2,1,0:T(8,128)(2,1)S(1)}, f32[3,640]{1,0:T(4,128)S(1)}) custom-call(bf16[2048,640]{1,0:T(8,128)(2,1)S(1)} %copy-done, bf16[2048,640]{1,0:T(8,128)(2,1)S(1)} %copy-done.1, f32[2,2048]{1,0:T(2,128)S(1)} %bitcast.21, bf16[3,80,640]{2,1,0:T(8,128)(2,1)S(1)} %collective-permute-done.refs_0_), custom_call_target="tpu_custom_call" | custom-call | flops 3019898880 | bytes 5242880 | tf_op jit(solution)/shard_map/update/pallas_call | solution.py:95
  39.6 2.4 %collective-permute-start.3 = (bf16[3,80,640]{2,1,0:T(8,128)(2,1)S(1)}, bf16[3,80,640]{2,1,0:T(8,128)(2,1)S(1)}, u32[]{:S(2)}, u32[]{:S(2)}) collective-permute-start(bf16[3,80,640]{2,1,0:T(8,128)(2,1)S(1)} %get-tuple-element.23), channel_id=1, source_target_pairs={{0,128},{64,192},{128,0},{192,64},{1,129},{65,193},{129,1},{193,65... | collective-permute-start | bytes 921608 | tf_op jit(solution)/shard_map/ppermute | solution.py:25
  42.0 5.1 %update.5 = (bf16[3,80,640]{2,1,0:T(8,128)(2,1)S(1)}, bf16[3,80,640]{2,1,0:T(8,128)(2,1)S(1)}, f32[3,640]{1,0:T(4,128)S(1)}) custom-call(bf16[2048,640]{1,0:T(8,128)(2,1)S(1)} %copy-done, bf16[2048,640]{1,0:T(8,128)(2,1)S(1)} %copy-done.1, f32[2,2048]{1,0:T(2,128)S(1)} %bitcast.22, bf16[3,80,640]{2,1,0:T(8,128)(2,1)S(1)} %collective-permute-done.1.refs_0_, ...), custom_call_target="tpu_custom_call" | custom-call | flops 6039797760 | bytes 5242880 | tf_op jit(solution)/shard_map/update/pallas_call | solution.py:95
  47.2 2.0 %collective-permute-start.5 = (bf16[3,80,640]{2,1,0:T(8,128)(2,1)S(1)}, bf16[3,80,640]{2,1,0:T(8,128)(2,1)S(1)}, u32[]{:S(2)}, u32[]{:S(2)}) collective-permute-start(bf16[3,80,640]{2,1,0:T(8,128)(2,1)S(1)} %get-tuple-element.28), channel_id=1, source_target_pairs={{0,192},{64,0},{128,64},{192,128},{1,193},{65,1},{129,65},{193,129... | collective-permute-start | bytes 921608 | tf_op jit(solution)/shard_map/ppermute | solution.py:25
  49.3 5.7 %collective-permute-done.4 = bf16[3,80,640]{2,1,0:T(8,128)(2,1)S(1)} collective-permute-done((bf16[3,80,640]{2,1,0:T(8,128)(2,1)S(1)}, bf16[3,80,640]{2,1,0:T(8,128)(2,1)S(1)}, u32[]{:S(2)}, u32[]{:S(2)}) %collective-permute-start.4) | collective-permute-done | bytes 307232 | tf_op jit(solution)/shard_map/ppermute | solution.py:25
  55.5 15.3 %all_to_all.16 = bf16[8,30,640]{2,1,0:T(8,128)(2,1)S(1)} all-to-all(bf16[8,30,640]{2,1,0:T(8,128)(2,1)S(1)} %copy.20), channel_id=1, replica_groups=mesh['x'=4,'z'=8,'y'=4,'core'=2] {'z'}, dimensions={0} | all-to-all | bytes 614400 | tf_op jit(solution)/shard_map/all_to_all | solution.py:278
  70.9 14.3 %all_to_all.17 = bf16[8,30,640]{2,1,0:T(8,128)(2,1)S(1)} all-to-all(bf16[8,30,640]{2,1,0:T(8,128)(2,1)S(1)} %broadcast_in_dim.2), channel_id=1, replica_groups=mesh['x'=4,'z'=8,'y'=4,'core'=2] {'z'}, dimensions={0} | all-to-all | bytes 614400 | tf_op jit(solution)/shard_map/all_to_all | solution.py:29
  85.5 1.3 %collective-permute-start.8 = (bf16[3,80,640]{2,1,0:T(8,128)(2,1)S(1)}, bf16[3,80,640]{2,1,0:T(8,128)(2,1)S(1)}, u32[]{:S(2)}, u32[]{:S(2)}) collective-permute-start(bf16[3,80,640]{2,1,0:T(8,128)(2,1)S(1)} %reshape.61.refs_0_), channel_id=1, source_target_pairs={{0,128},{64,192},{128,0},{192,64},{1,129},{65,193},{129,1},{193,65... | collective-permute-start | bytes 921608 | tf_op jit(solution)/shard_map/ppermute | solution.py:25
  86.7 2.0 %collective-permute-start.6 = (bf16[3,80,640]{2,1,0:T(8,128)(2,1)S(1)}, bf16[3,80,640]{2,1,0:T(8,128)(2,1)}, u32[]{:S(2)}, u32[]{:S(2)}) collective-permute-start(bf16[3,80,640]{2,1,0:T(8,128)(2,1)S(1)} %reshape.61.refs_0_), channel_id=1, source_target_pairs={{0,192},{64,0},{128,64},{192,128},{1,193},{65,1},{129,65},{193,129... | collective-permute-start | bytes 921608 | tf_op jit(solution)/shard_map/ppermute | solution.py:25
  88.8 7.0 %collective-permute-done.8.refs_3_ = bf16[3,80,640]{2,1,0:T(8,128)(2,1)S(1)} collective-permute-done((bf16[3,80,640]{2,1,0:T(8,128)(2,1)S(1)}, bf16[3,80,640]{2,1,0:T(8,128)(2,1)S(1)}, u32[]{:S(2)}, u32[]{:S(2)}) %collective-permute-start.8) | collective-permute-done | bytes 307232 | tf_op jit(solution)/shard_map/ppermute | solution.py:25
  95.8 2.7 %collective-permute-done.7.refs_2_ = bf16[3,80,640]{2,1,0:T(8,128)(2,1)S(1)} collective-permute-done((bf16[3,80,640]{2,1,0:T(8,128)(2,1)S(1)}, bf16[3,80,640]{2,1,0:T(8,128)(2,1)S(1)}, u32[]{:S(2)}, u32[]{:S(2)}) %collective-permute-start.7) | collective-permute-done | bytes 307232 | tf_op jit(solution)/shard_map/ppermute | solution.py:25
  99.1 8.6 %apply.1 = (bf16[2048,640]{1,0:T(8,128)(2,1)S(1)}, f32[16,128]{1,0:T(8,128)S(1)}, f32[3,640]{1,0:T(4,128)S(1)}) custom-call(bf16[2048,640]{1,0:T(8,128)(2,1)} %q_in.1, f32[3,640]{1,0:T(4,128)S(1)} %add_add_fusion.osq_ref, bf16[3,80,640]{2,1,0:T(8,128)(2,1)S(1)} %reshape.61.refs_0_, bf16[3,80,640]{2,1,0:T(8,128)(2,1)} %collective-permute-done.6.refs_1_, ...), custom_call_target="tpu_custom_call" | custom-call | flops 3019898880 | bytes 7864320 | tf_op jit(solution)/shard_map/apply/pallas_call | solution.py:179
  107.8 1.1 collective-permute-done.9
  109.0 1.6 %collective-permute-start.12 = (f32[2048]{0:T(1024)S(1)}, f32[2048]{0:T(1024)S(1)}, u32[]{:S(2)}, u32[]{:S(2)}) collective-permute-start(f32[2048]{0:T(1024)S(1)} %bitcast_add_fusion), channel_id=1, source_target_pairs={{0,2},{2,4},{4,6},{6,0},{1,3},{3,5},{5,7},{7,1},{8,10},{10,12},{12... | collective-permute-start | bytes 24584 | tf_op jit(solution)/shard_map/ppermute | solution.py:25
  110.6 1.6 %collective-permute-start.11 = (f32[2048]{0:T(1024)S(1)}, f32[2048]{0:T(1024)S(1)}, u32[]{:S(2)}, u32[]{:S(2)}) collective-permute-start(f32[2048]{0:T(1024)S(1)} %bitcast_add_fusion), channel_id=1, source_target_pairs={{0,6},{2,0},{4,2},{6,4},{1,7},{3,1},{5,3},{7,5},{8,14},{10,8},{12,... | collective-permute-start | bytes 24584 | tf_op jit(solution)/shard_map/ppermute | solution.py:25
  112.2 2.0 %collective-permute-start.10 = (f32[2048]{0:T(1024)S(1)}, f32[2048]{0:T(1024)S(1)}, u32[]{:S(2)}, u32[]{:S(2)}) collective-permute-start(f32[2048]{0:T(1024)S(1)} %bitcast_add_fusion), channel_id=1, source_target_pairs={{0,4},{2,6},{4,0},{6,2},{1,5},{3,7},{5,1},{7,3},{8,12},{10,14},{12... | collective-permute-start | bytes 24584 | tf_op jit(solution)/shard_map/ppermute | solution.py:25
  117.4 1.7 %scale.1 = bf16[2048,640]{1,0:T(8,128)(2,1)} custom-call(bf16[2048,640]{1,0:T(8,128)(2,1)S(1)} %get-tuple-element.29.o_ref, f32[1,640]{1,0:T(1,128)S(1)} %reshape.62.gain_ref, f32[16,128]{1,0:T(8,128)S(1)} %bitcast.15, f32[16,128]{1,0:T(8,128)S(1)} %bitcast.18, f32[16,128]{1,0:T(8,128)S(1)} %bitcast.17, f32[16,128]{1,0:T(8,128)S(1)} %bitcast.16), custom_call_target="tpu_custom_call" | custom-call | tf_op jit(solution)/shard_map/scale/pallas_call | solution.py:228
  (46 shorter events, 5.1 us)
Async XLA Ops:
  0.6 28.0 %copy-start = (bf16[2048,640]{1,0:T(8,128)(2,1)S(1)}, bf16[2048,640]{1,0:T(8,128)(2,1)}, u32[]{:S(2)}) copy-start(bf16[2048,640]{1,0:T(8,128)(2,1)} %k_ref.5) | copy-start | bytes 7864324
  0.6 28.0 %copy-start.2 = (f32[2048,2]{0,1:T(2,128)S(1)}, f32[2048,2]{0,1:T(2,128)}, u32[]{:S(2)}) copy-start(f32[2048,2]{0,1:T(2,128)} %param.11) | copy-start | bytes 49156
  24.4 11.8 %collective-permute-start = (bf16[3,80,640]{2,1,0:T(8,128)(2,1)S(1)}, bf16[3,80,640]{2,1,0:T(8,128)(2,1)S(1)}, u32[]{:S(2)}, u32[]{:S(2)}) collective-permute-start(bf16[3,80,640]{2,1,0:T(8,128)(2,1)S(1)} %reshape.57.refs_0_), channel_id=1, source_target_pairs={{0,128},{64,192},{128,0},{192,64},{1,129},{65,193},{129,1},{193,65... | collective-permute-start | bytes 921608 | tf_op jit(solution)/shard_map/ppermute | solution.py:25
  26.6 15.4 %collective-permute-start.2 = (bf16[3,80,640]{2,1,0:T(8,128)(2,1)S(1)}, bf16[3,80,640]{2,1,0:T(8,128)(2,1)S(1)}, u32[]{:S(2)}, u32[]{:S(2)}) collective-permute-start(bf16[3,80,640]{2,1,0:T(8,128)(2,1)S(1)} %reshape.57.refs_0_), channel_id=1, source_target_pairs={{0,64},{64,128},{128,192},{192,0},{1,65},{65,129},{129,193},{193,1... | collective-permute-start | bytes 921608 | tf_op jit(solution)/shard_map/ppermute | solution.py:25
  26.6 15.4 %collective-permute-start.1 = (bf16[3,80,640]{2,1,0:T(8,128)(2,1)S(1)}, bf16[3,80,640]{2,1,0:T(8,128)(2,1)S(1)}, u32[]{:S(2)}, u32[]{:S(2)}) collective-permute-start(bf16[3,80,640]{2,1,0:T(8,128)(2,1)S(1)} %reshape.57.refs_0_), channel_id=1, source_target_pairs={{0,192},{64,0},{128,64},{192,128},{1,193},{65,1},{129,65},{193,129... | collective-permute-start | bytes 921608 | tf_op jit(solution)/shard_map/ppermute | solution.py:25
  28.7 1.7 %copy-start.1 = (bf16[2048,640]{1,0:T(8,128)(2,1)S(1)}, bf16[2048,640]{1,0:T(8,128)(2,1)}, u32[]{:S(2)}) copy-start(bf16[2048,640]{1,0:T(8,128)(2,1)} %v_ref.5) | copy-start | bytes 7864324
  39.6 9.6 %collective-permute-start.3 = (bf16[3,80,640]{2,1,0:T(8,128)(2,1)S(1)}, bf16[3,80,640]{2,1,0:T(8,128)(2,1)S(1)}, u32[]{:S(2)}, u32[]{:S(2)}) collective-permute-start(bf16[3,80,640]{2,1,0:T(8,128)(2,1)S(1)} %get-tuple-element.23), channel_id=1, source_target_pairs={{0,128},{64,192},{128,0},{192,64},{1,129},{65,193},{129,1},{193,65... | collective-permute-start | bytes 921608 | tf_op jit(solution)/shard_map/ppermute | solution.py:25
  47.1 7.9 %collective-permute-start.4 = (bf16[3,80,640]{2,1,0:T(8,128)(2,1)S(1)}, bf16[3,80,640]{2,1,0:T(8,128)(2,1)S(1)}, u32[]{:S(2)}, u32[]{:S(2)}) collective-permute-start(bf16[3,80,640]{2,1,0:T(8,128)(2,1)S(1)} %get-tuple-element.27), channel_id=1, source_target_pairs={{0,64},{64,128},{128,192},{192,0},{1,65},{65,129},{129,193},{193,1... | collective-permute-start | bytes 921608 | tf_op jit(solution)/shard_map/ppermute | solution.py:25
  47.2 7.9 %collective-permute-start.5 = (bf16[3,80,640]{2,1,0:T(8,128)(2,1)S(1)}, bf16[3,80,640]{2,1,0:T(8,128)(2,1)S(1)}, u32[]{:S(2)}, u32[]{:S(2)}) collective-permute-start(bf16[3,80,640]{2,1,0:T(8,128)(2,1)S(1)} %get-tuple-element.28), channel_id=1, source_target_pairs={{0,192},{64,0},{128,64},{192,128},{1,193},{65,1},{129,65},{193,129... | collective-permute-start | bytes 921608 | tf_op jit(solution)/shard_map/ppermute | solution.py:25
  49.3 21.5 %copy-start.3 = (bf16[30,640]{1,0:T(8,128)(2,1)S(1)}, bf16[30,640]{1,0:T(8,128)(2,1)}, u32[]{:S(2)}) copy-start(bf16[30,640]{1,0:T(8,128)(2,1)} %get-tuple-element.26) | copy-start | bytes 115204
  55.4 33.3 %copy-start.4 = (f32[640]{0:T(1024)S(1)}, f32[640]{0:T(1024)}, u32[]{:S(2)}) copy-start(f32[640]{0:T(1024)} %param.15) | copy-start | bytes 7684
  85.5 10.4 %collective-permute-start.8 = (bf16[3,80,640]{2,1,0:T(8,128)(2,1)S(1)}, bf16[3,80,640]{2,1,0:T(8,128)(2,1)S(1)}, u32[]{:S(2)}, u32[]{:S(2)}) collective-permute-start(bf16[3,80,640]{2,1,0:T(8,128)(2,1)S(1)} %reshape.61.refs_0_), channel_id=1, source_target_pairs={{0,128},{64,192},{128,0},{192,64},{1,129},{65,193},{129,1},{193,65... | collective-permute-start | bytes 921608 | tf_op jit(solution)/shard_map/ppermute | solution.py:25
  86.7 11.8 %collective-permute-start.7 = (bf16[3,80,640]{2,1,0:T(8,128)(2,1)S(1)}, bf16[3,80,640]{2,1,0:T(8,128)(2,1)S(1)}, u32[]{:S(2)}, u32[]{:S(2)}) collective-permute-start(bf16[3,80,640]{2,1,0:T(8,128)(2,1)S(1)} %reshape.61.refs_0_), channel_id=1, source_target_pairs={{0,64},{64,128},{128,192},{192,0},{1,65},{65,129},{129,193},{193,1... | collective-permute-start | bytes 921608 | tf_op jit(solution)/shard_map/ppermute | solution.py:25
  86.7 12.3 %collective-permute-start.6 = (bf16[3,80,640]{2,1,0:T(8,128)(2,1)S(1)}, bf16[3,80,640]{2,1,0:T(8,128)(2,1)}, u32[]{:S(2)}, u32[]{:S(2)}) collective-permute-start(bf16[3,80,640]{2,1,0:T(8,128)(2,1)S(1)} %reshape.61.refs_0_), channel_id=1, source_target_pairs={{0,192},{64,0},{128,64},{192,128},{1,193},{65,1},{129,65},{193,129... | collective-permute-start | bytes 921608 | tf_op jit(solution)/shard_map/ppermute | solution.py:25
  95.8 2.7 %copy-start.5 = (bf16[3,80,640]{2,1,0:T(8,128)(2,1)}, bf16[3,80,640]{2,1,0:T(8,128)(2,1)S(1)}, u32[]{:S(2)}) copy-start(bf16[3,80,640]{2,1,0:T(8,128)(2,1)S(1)} %collective-permute-done.8.refs_3_) | copy-start | bytes 921604
  107.7 1.3 %collective-permute-start.9 = (f32[2048]{0:T(1024)S(1)}, f32[2048]{0:T(1024)S(1)}, u32[]{:S(2)}, u32[]{:S(2)}) collective-permute-start(f32[2048]{0:T(1024)S(1)} %bitcast.19), channel_id=1, source_target_pairs={{0,1},{1,0},{2,3},{3,2},{4,5},{5,4},{6,7},{7,6},{8,9},{9,8},{10,11... | collective-permute-start | bytes 24584 | tf_op jit(solution)/shard_map/ppermute | solution.py:25
  109.0 7.3 %collective-permute-start.12 = (f32[2048]{0:T(1024)S(1)}, f32[2048]{0:T(1024)S(1)}, u32[]{:S(2)}, u32[]{:S(2)}) collective-permute-start(f32[2048]{0:T(1024)S(1)} %bitcast_add_fusion), channel_id=1, source_target_pairs={{0,2},{2,4},{4,6},{6,0},{1,3},{3,5},{5,7},{7,1},{8,10},{10,12},{12... | collective-permute-start | bytes 24584 | tf_op jit(solution)/shard_map/ppermute | solution.py:25
  110.6 5.7 %collective-permute-start.11 = (f32[2048]{0:T(1024)S(1)}, f32[2048]{0:T(1024)S(1)}, u32[]{:S(2)}, u32[]{:S(2)}) collective-permute-start(f32[2048]{0:T(1024)S(1)} %bitcast_add_fusion), channel_id=1, source_target_pairs={{0,6},{2,0},{4,2},{6,4},{1,7},{3,1},{5,3},{7,5},{8,14},{10,8},{12,... | collective-permute-start | bytes 24584 | tf_op jit(solution)/shard_map/ppermute | solution.py:25
  112.2 5.2 %collective-permute-start.10 = (f32[2048]{0:T(1024)S(1)}, f32[2048]{0:T(1024)S(1)}, u32[]{:S(2)}, u32[]{:S(2)}) collective-permute-start(f32[2048]{0:T(1024)S(1)} %bitcast_add_fusion), channel_id=1, source_target_pairs={{0,4},{2,6},{4,0},{6,2},{1,5},{3,7},{5,1},{7,3},{8,12},{10,14},{12... | collective-permute-start | bytes 24584 | tf_op jit(solution)/shard_map/ppermute | solution.py:25
